TPU v7x, 32 devices: a whole 2x2x4 slice. The times are simulated.
32 devices in a mesh: band: 4 (over y, core), seq: 8 (over z, x).
Axes of the slice: x: 2, y: 2, z: 4, core: 2. Of those that a mesh axis runs over, the one named last changes fastest.
Arguments:
- frames: bfloat16 [4, 1024, 768], P('band', 'seq'), may hold values from -6 to 6
- text: bfloat16 [4, 128, 768], P('band'), may hold values from -6 to 6
- timesteps: int32 [4], P('band'), may hold values from 0 to 999
- frame_lengths: int32 [4], P('band'), may hold values from 128 to 1024, as said below
- text_mask: int32 [4, 128], P('band'), may hold values from 0 to 1, as said below
- cotangent: bfloat16 [4, 1024, 768], P('band', 'seq'), may hold values from -6 to 6
- w_time_in: bfloat16 [256, 768], replicated, may hold values from -0.5 to 0.5
- w_time_out: bfloat16 [768, 768], replicated, may hold values from -0.3125 to 0.3125
- w_adaln: bfloat16 [768, 4608], replicated, may hold values from -0.4375 to 0.4375
- w_query: bfloat16 [768, 768], replicated, may hold values from -0.21875 to 0.21875
- w_key: bfloat16 [768, 768], replicated, may hold values from -0.21875 to 0.21875
- w_value: bfloat16 [768, 768], replicated, may hold values from -0.21875 to 0.21875
- w_attn_out: bfloat16 [768, 768], replicated, may hold values from -4 to 4
- cross_gain: bfloat16 [768], replicated, may hold values from 0.25 to 1.75
- w_cross_query: bfloat16 [768, 768], replicated, may hold values from -0.21875 to 0.21875
- w_cross_key: bfloat16 [768, 768], replicated, may hold values from -0.21875 to 0.21875
- w_cross_value: bfloat16 [768, 768], replicated, may hold values from -0.21875 to 0.21875
- w_cross_out: bfloat16 [768, 768], replicated, may hold values from -1 to 1
- w_mlp_in: bfloat16 [768, 3072], replicated, may hold values from -0.21875 to 0.21875
- w_mlp_out: bfloat16 [3072, 768], replicated, may hold values from -0.109375 to 0.109375
Outputs:
- block_out: bfloat16 [4, 1024, 768], P('band', 'seq')
- grad_frames: bfloat16 [4, 1024, 768], P('band', 'seq')
- grad_text: float32 [4, 128, 768], P('band', 'seq')
- grad_w_time_in: float32 [256, 768], P(None, 'seq')
- grad_w_time_out: float32 [768, 768], P(None, 'seq')
- grad_w_adaln: float32 [768, 4608], P(None, 'seq')
- grad_w_query: float32 [768, 768], P(None, 'seq')
- grad_w_key: float32 [768, 768], P(None, 'seq')
- grad_w_value: float32 [768, 768], P(None, 'seq')
- grad_w_attn_out: float32 [768, 768], P(None, 'seq')
- grad_cross_gain: float32 [768], P('seq')
- grad_w_cross_query: float32 [768, 768], P(None, 'seq')
- grad_w_cross_key: float32 [768, 768], P(None, 'seq')
- grad_w_cross_value: float32 [768, 768], P(None, 'seq')
- grad_w_cross_out: float32 [768, 768], P(None, 'seq')
- grad_w_mlp_in: float32 [768, 3072], P(None, 'seq')
- grad_w_mlp_out: float32 [3072, 768], P(None, 'seq')
Inputs may be any that keep to these rules, and one draw needn't show every extreme that they name: `frame_lengths`: in every draw some clip has all 1024 frames valid. `text_mask`: the first text token of every clip is real.
All inputs are finite; a program needn't handle non-finite values.
Results may differ from a plain program's by a relative error of at most 0.029.
Values may be sent and summed in bfloat16 or wider, within the bound.
A program may use at most 256 MiB of HBM per device.

v0:
```python
import math

import jax
import jax.numpy as jnp
from jax import lax
from jax.sharding import PartitionSpec as P

H = 12
HD = 64


epsilon = 1e-06
masked_value = -1000000000.0
key_block = 512


def for_sending(value):
    return jax.tree.map(lambda a: a.astype(jnp.bfloat16) if a.dtype == jnp.float32 else a, value)


def narrow(values):
    return values.astype(jnp.bfloat16)


def product(left, right):
    return jnp.dot(left, right, preferred_element_type=jnp.float32)


def transposed_left(left, right):
    return lax.dot_general(
        left, right, (((0,), (0,)), ((), ())), preferred_element_type=jnp.float32
    )


def transposed_right(left, right):
    return lax.dot_general(
        left, right, (((1,), (1,)), ((), ())), preferred_element_type=jnp.float32
    )


def layer_norm(inputs):
    center = inputs - jnp.mean(inputs, axis=-1, keepdims=True)
    scaling = lax.rsqrt(jnp.mean(center * center, axis=-1, keepdims=True) + epsilon)
    return (center * scaling, scaling)


def norm_back(normed, scaling, gradient):
    mean_grad = jnp.mean(gradient, axis=-1, keepdims=True)
    mean_prod = jnp.mean(gradient * normed, axis=-1, keepdims=True)
    return scaling * (gradient - mean_grad - normed * mean_prod)


def time_embed(timesteps, width):
    half_width = width // 2
    frequency = jnp.exp(-math.log(10000.0) * jnp.arange(half_width, dtype=jnp.float32) / half_width)
    angles = timesteps.astype(jnp.float32)[:, None] * frequency[None, :]
    return jnp.concatenate([jnp.cos(angles), jnp.sin(angles)], axis=1)


def split_heads(rows_in):
    return rows_in.reshape(rows_in.shape[0], rows_in.shape[1], H, HD)


def masked_scores(queries, key_rows, key_valid):
    scores = (
        jnp.einsum("cqhd,ckhd->cqhk", queries, key_rows, preferred_element_type=jnp.float32) * 0.125
    )
    return jnp.where(key_valid[:, None, None, :], scores, masked_value)


def block_valid(anchor, start_row, block_size, lengths):
    return (anchor + start_row + jnp.arange(block_size))[None, :] < lengths[:, None]


def forward_piece(running, segment, anchor, queries, lengths):
    row_count = segment.shape[1]
    block_size = math.gcd(row_count, key_block)
    width = queries.shape[2] * queries.shape[3]

    def forward_one_block(running, counter):
        rows_in = lax.dynamic_slice_in_dim(segment, counter * block_size, block_size, 1)
        key_valid = block_valid(anchor, counter * block_size, block_size, lengths)
        scores = masked_scores(queries, split_heads(rows_in[:, :, :width]), key_valid)
        row_max, row_sum, weighted = running
        new_max = jnp.maximum(row_max, jnp.max(scores, axis=-1))
        factor = jnp.exp(row_max - new_max)
        expanded = jnp.exp(scores - new_max[..., None])
        row_sum = row_sum * factor + jnp.sum(expanded, axis=-1)
        weighted = weighted * factor[..., None] + jnp.einsum(
            "cqhk,ckhd->cqhd",
            narrow(expanded),
            split_heads(rows_in[:, :, width:]),
            preferred_element_type=jnp.float32,
        )
        return ((new_max, row_sum, weighted), None)

    running, unused = lax.scan(forward_one_block, running, jnp.arange(row_count // block_size))
    return running


def query_piece(gradient, segment, anchor, queries, grad_heads, log_total, row_delta, lengths):
    row_count = segment.shape[1]
    block_size = math.gcd(row_count, key_block)
    width = queries.shape[2] * queries.shape[3]

    def query_one_block(gradient, counter):
        rows_in = lax.dynamic_slice_in_dim(segment, counter * block_size, block_size, 1)
        key_valid = block_valid(anchor, counter * block_size, block_size, lengths)
        key_rows = split_heads(rows_in[:, :, :width])
        scores = masked_scores(queries, key_rows, key_valid)
        attn_probs = jnp.exp(scores - log_total[..., None])
        grad_probs = jnp.einsum(
            "cqhd,ckhd->cqhk",
            grad_heads,
            split_heads(rows_in[:, :, width:]),
            preferred_element_type=jnp.float32,
        )
        grad_scores = narrow(attn_probs * (grad_probs - row_delta[..., None]))
        gradient = (
            gradient
            + jnp.einsum(
                "cqhk,ckhd->cqhd", grad_scores, key_rows, preferred_element_type=jnp.float32
            )
            * 0.125
        )
        return (gradient, None)

    gradient, unused = lax.scan(query_one_block, gradient, jnp.arange(row_count // block_size))
    return gradient


def own_columns(values, place, count):
    share = values.shape[1] // count
    return lax.dynamic_slice_in_dim(values, place * share, share, 1)


def on_device(
    frames,
    text,
    timesteps,
    frame_lengths,
    text_mask,
    cotangent,
    w_time_in,
    w_time_out,
    w_adaln,
    w_query,
    w_key,
    w_value,
    w_attn_out,
    cross_gain,
    w_cross_query,
    w_cross_key,
    w_cross_value,
    w_cross_out,
    w_mlp_in,
    w_mlp_out,
):
    clips = frames.shape[0]
    rows = frames.shape[1]
    width = frames.shape[2]
    tokens = clips * rows
    text_count = text.shape[1]
    seq_place = lax.axis_index("seq")
    seq_count = lax.axis_size("seq")
    offset = seq_place * rows
    inputs = frames.astype(jnp.float32)
    own_valid = (offset + jnp.arange(rows))[None, :] < frame_lengths[:, None]
    row_valid = own_valid[:, :, None]
    text_valid = text_mask != 0

    def flatten(values):
        return values.reshape(tokens, values.shape[-1])

    def unflatten(values):
        return values.reshape(clips, rows, values.shape[-1])

    time_vector = narrow(time_embed(timesteps, w_time_in.shape[0]))
    time_first = product(time_vector, w_time_in)
    time_hidden = narrow(jax.nn.silu(time_first))
    time_out = product(time_hidden, w_time_out)
    condition = narrow(jax.nn.silu(time_out))
    modulation = product(condition, w_adaln)
    shift_attn, scale_attn, gate_attn, shift_mlp, scale_mlp, gate_mlp = [
        piece[:, None, :] for piece in jnp.split(modulation, 6, axis=1)
    ]
    normed_attn, scaling_attn = layer_norm(inputs)
    attn_in = narrow(normed_attn * (1.0 + scale_attn) + shift_attn)
    attn_flat = flatten(attn_in)
    query_flat = narrow(product(attn_flat, w_query))
    queries = split_heads(unflatten(query_flat))
    kv_local = unflatten(
        jnp.concatenate(
            [narrow(product(attn_flat, w_key)), narrow(product(attn_flat, w_value))], axis=1
        )
    )
    start_state = (
        jnp.full((clips, rows, H), -1e30, jnp.float32),
        jnp.zeros((clips, rows, H), jnp.float32),
        jnp.zeros((clips, rows, H, HD), jnp.float32),
    )
    row_max, row_sum, weighted = forward_piece(
        start_state,
        lax.all_gather(kv_local, "seq", axis=1, tiled=True),
        jnp.int32(0),
        queries,
        frame_lengths,
    )
    attended = weighted / row_sum[..., None]
    log_total = row_max + jnp.log(row_sum)
    attn_low = narrow(attended.reshape(clips, rows, width))
    attn_proj = unflatten(product(flatten(attn_low), w_attn_out))
    middle = inputs + gate_attn * attn_proj
    normed_cross, scaling_cross = layer_norm(middle)
    gain_values = cross_gain.astype(jnp.float32)
    cross_in = narrow(normed_cross * gain_values)
    cross_queries = split_heads(unflatten(narrow(product(flatten(cross_in), w_cross_query))))
    text_flat = text.reshape(clips * text_count, width)
    cross_keys = split_heads(
        narrow(product(text_flat, w_cross_key)).reshape(clips, text_count, width)
    )
    cross_values = split_heads(
        narrow(product(text_flat, w_cross_value)).reshape(clips, text_count, width)
    )
    cross_scores = masked_scores(cross_queries, cross_keys, text_valid)
    cross_max = jnp.max(cross_scores, axis=-1, keepdims=True)
    cross_total = cross_max + jnp.log(
        jnp.sum(jnp.exp(cross_scores - cross_max), axis=-1, keepdims=True)
    )
    cross_probs = jnp.exp(cross_scores - cross_total)
    cross_probs_low = narrow(cross_probs)
    cross_attended = jnp.einsum(
        "cqhk,ckhd->cqhd", cross_probs_low, cross_values, preferred_element_type=jnp.float32
    )
    cross_low = narrow(cross_attended.reshape(clips, rows, width))
    after_cross = middle + unflatten(product(flatten(cross_low), w_cross_out))
    normed_mlp, scaling_mlp = layer_norm(after_cross)
    mlp_in = narrow(normed_mlp * (1.0 + scale_mlp) + shift_mlp)
    pre_act = product(flatten(mlp_in), w_mlp_in)
    activation = narrow(jax.nn.gelu(pre_act, approximate=True))
    mlp_out = unflatten(product(activation, w_mlp_out))
    result = after_cross + gate_mlp * mlp_out
    block_out = jnp.where(row_valid, result, inputs).astype(jnp.bfloat16)
    grad_out = cotangent.astype(jnp.float32)
    grad_res = jnp.where(row_valid, grad_out, 0.0)
    grad_mlp = flatten(narrow(gate_mlp * grad_res))
    grad_w_mlp_out = transposed_left(activation, grad_mlp)
    grad_act = transposed_right(grad_mlp, w_mlp_out)
    gelu_pull = jax.vjp(lambda values: jax.nn.gelu(values, approximate=True), pre_act)[1]
    grad_pre = narrow(gelu_pull(grad_act)[0])
    grad_w_mlp_in = transposed_left(flatten(mlp_in), grad_pre)
    grad_mlp_in = unflatten(transposed_right(grad_pre, w_mlp_in))
    grad_after = grad_res + norm_back(normed_mlp, scaling_mlp, grad_mlp_in * (1.0 + scale_mlp))
    grad_cross_out = flatten(narrow(grad_after))
    grad_w_cross_out = transposed_left(flatten(cross_low), grad_cross_out)
    grad_cross_attn = split_heads(unflatten(narrow(transposed_right(grad_cross_out, w_cross_out))))
    cross_delta = jnp.sum(grad_cross_attn.astype(jnp.float32) * cross_attended, axis=-1)
    cross_grad_probs = jnp.einsum(
        "cqhd,ckhd->cqhk", grad_cross_attn, cross_values, preferred_element_type=jnp.float32
    )
    cross_grad_scores = narrow(cross_probs * (cross_grad_probs - cross_delta[..., None]))
    grad_cross_query = narrow(
        jnp.einsum(
            "cqhk,ckhd->cqhd", cross_grad_scores, cross_keys, preferred_element_type=jnp.float32
        )
        * 0.125
    ).reshape(tokens, width)
    cross_key_part = (
        jnp.einsum(
            "cqhk,cqhd->ckhd", cross_grad_scores, cross_queries, preferred_element_type=jnp.float32
        )
        * 0.125
    )
    cross_value_part = jnp.einsum(
        "cqhk,cqhd->ckhd", cross_probs_low, grad_cross_attn, preferred_element_type=jnp.float32
    )
    cross_kv_part = jnp.concatenate(
        [
            cross_key_part.reshape(clips, text_count, width),
            cross_value_part.reshape(clips, text_count, width),
        ],
        axis=2,
    )
    text_total = lax.psum_scatter(cross_kv_part, "seq", scatter_dimension=1, tiled=True)
    text_share = text_total.shape[1]
    grad_cross_key = narrow(text_total[:, :, :width]).reshape(clips * text_share, width)
    grad_cross_value = narrow(text_total[:, :, width:]).reshape(clips * text_share, width)
    text_own = lax.dynamic_slice_in_dim(text, seq_place * text_share, text_share, 1).reshape(
        clips * text_share, width
    )
    grad_text = (
        transposed_right(grad_cross_key, w_cross_key)
        + transposed_right(grad_cross_value, w_cross_value)
    ).reshape(clips, text_share, width)
    grad_w_cross_key = transposed_left(text_own, grad_cross_key)
    grad_w_cross_value = transposed_left(text_own, grad_cross_value)
    grad_w_cross_query = transposed_left(flatten(cross_in), grad_cross_query)
    grad_cross_in = unflatten(transposed_right(grad_cross_query, w_cross_query))
    grad_gain_part = jnp.sum(grad_cross_in * normed_cross, axis=(0, 1))
    grad_mid = grad_after + norm_back(normed_cross, scaling_cross, grad_cross_in * gain_values)
    grad_attn_proj = flatten(narrow(gate_attn * grad_mid))
    grad_w_attn_out = transposed_left(flatten(attn_low), grad_attn_proj)
    grad_attn_flat = narrow(transposed_right(grad_attn_proj, w_attn_out))
    grad_heads = split_heads(unflatten(grad_attn_flat))
    row_delta = jnp.sum(grad_heads.astype(jnp.float32) * attended, axis=-1)
    zero_heads = jnp.zeros((clips, rows, H, HD), jnp.float32)
    gathered = lax.all_gather(kv_local, "seq", axis=1, tiled=True)
    query_grad = query_piece(
        zero_heads, gathered, 0, queries, grad_heads, log_total, row_delta, frame_lengths
    )
    anchor = jnp.int32(0)
    block_size = math.gcd(rows * lax.axis_size("seq"), key_block)

    def key_one_block(counter):
        rows_in = lax.dynamic_slice_in_dim(gathered, counter * block_size, block_size, 1)
        key_valid = block_valid(anchor, counter * block_size, block_size, frame_lengths)
        scores = masked_scores(queries, split_heads(rows_in[:, :, :width]), key_valid)
        attn_probs = jnp.exp(scores - log_total[..., None])
        grad_probs = jnp.einsum(
            "cqhd,ckhd->cqhk",
            grad_heads,
            split_heads(rows_in[:, :, width:]),
            preferred_element_type=jnp.float32,
        )
        grad_scores = narrow(attn_probs * (grad_probs - row_delta[..., None]))
        grad_keys = (
            jnp.einsum("cqhk,cqhd->ckhd", grad_scores, queries, preferred_element_type=jnp.float32)
            * 0.125
        )
        grad_values = jnp.einsum(
            "cqhk,cqhd->ckhd", narrow(attn_probs), grad_heads, preferred_element_type=jnp.float32
        )
        joined = jnp.concatenate(
            [
                grad_keys.reshape(clips, block_size, width),
                grad_values.reshape(clips, block_size, width),
            ],
            axis=2,
        )
        return jnp.transpose(joined, (1, 0, 2))

    blocks = lax.map(key_one_block, jnp.arange(rows * lax.axis_size("seq") // block_size))
    kv_term = lax.psum_scatter(
        blocks.reshape(rows * lax.axis_size("seq"), clips, 2 * width),
        "seq",
        scatter_dimension=0,
        tiled=True,
    )
    kv_grad = jnp.transpose(kv_term, (1, 0, 2))
    grad_query = narrow(query_grad.reshape(tokens, width))
    grad_key = flatten(narrow(kv_grad[:, :, :width]))
    grad_value = flatten(narrow(kv_grad[:, :, width:]))
    grad_w_query = transposed_left(attn_flat, grad_query)
    grad_w_key = transposed_left(attn_flat, grad_key)
    grad_w_value = transposed_left(attn_flat, grad_value)
    grad_attn_in = unflatten(
        transposed_right(grad_query, w_query)
        + transposed_right(grad_key, w_key)
        + transposed_right(grad_value, w_value)
    )
    grad_inputs = grad_mid + norm_back(normed_attn, scaling_attn, grad_attn_in * (1.0 + scale_attn))
    grad_frames = jnp.where(row_valid, grad_inputs, grad_out).astype(jnp.bfloat16)
    modulation_part = jnp.concatenate(
        [
            jnp.sum(grad_attn_in, axis=1),
            jnp.sum(grad_attn_in * normed_attn, axis=1),
            jnp.sum(grad_mid * attn_proj, axis=1),
            jnp.sum(grad_mlp_in, axis=1),
            jnp.sum(grad_mlp_in * normed_mlp, axis=1),
            jnp.sum(grad_res * mlp_out, axis=1),
        ],
        axis=1,
    )
    modulation_total = lax.psum(modulation_part, "seq")
    grad_modulation = narrow(modulation_total)
    grad_w_adaln = transposed_left(condition, grad_modulation)
    grad_condition = transposed_right(grad_modulation, w_adaln)
    grad_time_out = narrow(jax.vjp(jax.nn.silu, time_out)[1](grad_condition)[0])
    grad_w_time_out = transposed_left(time_hidden, grad_time_out)
    grad_time_hidden = transposed_right(grad_time_out, w_time_out)
    grad_time_first = jax.vjp(jax.nn.silu, time_first)[1](grad_time_hidden)[0]
    grad_w_time_in = lax.dot_general(
        time_vector.astype(jnp.float32),
        grad_time_first,
        (((0,), (0,)), ((), ())),
        precision=lax.Precision.HIGHEST,
    )
    shared = (
        lax.psum_scatter(grad_w_query, "seq", scatter_dimension=1, tiled=True),
        lax.psum_scatter(grad_w_key, "seq", scatter_dimension=1, tiled=True),
        lax.psum_scatter(grad_w_value, "seq", scatter_dimension=1, tiled=True),
        lax.psum_scatter(grad_w_attn_out, "seq", scatter_dimension=1, tiled=True),
        lax.psum_scatter(grad_gain_part, "seq", scatter_dimension=0, tiled=True),
        lax.psum_scatter(grad_w_cross_query, "seq", scatter_dimension=1, tiled=True),
        lax.psum_scatter(grad_w_cross_key, "seq", scatter_dimension=1, tiled=True),
        lax.psum_scatter(grad_w_cross_value, "seq", scatter_dimension=1, tiled=True),
        lax.psum_scatter(grad_w_cross_out, "seq", scatter_dimension=1, tiled=True),
        lax.psum_scatter(grad_w_mlp_in, "seq", scatter_dimension=1, tiled=True),
        lax.psum_scatter(grad_w_mlp_out, "seq", scatter_dimension=1, tiled=True),
    )
    replicated = (
        own_columns(grad_w_time_in, seq_place, seq_count),
        own_columns(grad_w_time_out, seq_place, seq_count),
        own_columns(grad_w_adaln, seq_place, seq_count),
    )
    summed = jax.tree.map(
        lambda part: part.astype(jnp.float32), lax.psum(for_sending(shared + replicated), "band")
    )
    (
        sum_query,
        sum_key,
        sum_value,
        sum_attn_out,
        sum_gain,
        sum_cross_query,
        sum_cross_key,
        sum_cross_value,
        sum_cross_out,
        sum_mlp_in,
        sum_mlp_out,
        sum_time_in,
        sum_time_out,
        sum_adaln,
    ) = summed
    return (
        block_out,
        grad_frames,
        grad_text,
        sum_time_in,
        sum_time_out,
        sum_adaln,
        sum_query,
        sum_key,
        sum_value,
        sum_attn_out,
        sum_gain,
        sum_cross_query,
        sum_cross_key,
        sum_cross_value,
        sum_cross_out,
        sum_mlp_in,
        sum_mlp_out,
    )


def solution(mesh):
    placed = (
        P("band", "seq", None),
        P("band", None, None),
        P("band"),
        P("band"),
        P("band", None),
        P("band", "seq", None),
        P(),
        P(),
        P(),
        P(),
        P(),
        P(),
        P(),
        P(),
        P(),
        P(),
        P(),
        P(),
        P(),
        P(),
    )
    return jax.shard_map(
        on_device,
        mesh=mesh,
        in_specs=placed,
        out_specs=(
            P("band", "seq", None),
            P("band", "seq", None),
            P("band", "seq", None),
            P(None, "seq"),
            P(None, "seq"),
            P(None, "seq"),
            P(None, "seq"),
            P(None, "seq"),
            P(None, "seq"),
            P(None, "seq"),
            P("seq"),
            P(None, "seq"),
            P(None, "seq"),
            P(None, "seq"),
            P(None, "seq"),
            P(None, "seq"),
            P(None, "seq"),
        ),
        check_vma=False,
    )
```

profile of v0, /device:TPU:0, one launch (start us, length us, event | category | flops | bytes accessed | tf_op | source)
XLA Modules:
  0.0 1403.9 jit_solution(1781427693421363203)
XLA Ops:
  14.9 4.1 fusion.187
  31.4 53.0 %all-gather.3.cloned.1.call-done = bf16[1024,1536]{1,0:T(8,128)(2,1)} async-done(((bf16[128,1536]{1,0:T(8,128)(2,1)}), bf16[1024,1536]{1,0:T(8,128)(2,1)}) %all-gather.3.cloned.1.call-update) | async-done | bytes 3145744 | tf_op jit(solution)/shard_map/all_gather | solution.py:204
  84.4 4.8 copy.108
  89.2 12.2 while.37
  112.6 5.3 fusion.73
  134.3 34.7 %while.36 = (s32[]{:T(128)}, f32[2,512,1,1536]{3,1,0,2:T(8,128)}, s32[2]{0:T(128)S(1)}, s32[1]{0:T(128)}, bf16[1,1024,1536]{1,2,0:T(8,128)(2,1)}, /*index=5*/bf1...) while((s32[]{:T(128)}, f32[2,512,1,1536]{3,1,0,2:T(8,128)}, ...), condition=%wide.region_21.22_spmd, body=%wide.region_20.21_spmd.sunk | while | flops 411698176 | bytes 43273988 | solution.py:342
  156.7 4.1 fusion.280
  179.6 25.5 %while.38 = (s32[]{:T(128)}, f32[1,128,12,64]{1,3,2,0:T(8,128)}, s32[2]{0:T(128)}, bf16[1,1024,1536]{1,2,0:T(8,128)(2,1)S(1)}, s32[1]{0:T(128)}, /*index=5*/bf16...) while((s32[]{:T(128)}, f32[1,128,12,64]{1,3,2,0:T(8,128)}, ...), condition=%wide.region_19.20_spmd.clone, body=%wide.region_18.19_spmd.clone.sunk | while | flops 307004416 | bytes 12989677 | solution.py:128
  187.5 4.8 fusion.294
  200.1 5.0 fusion.294
  213.5 72.4 %reduce-scatter.12.cloned.1.call-done = f32[128,1,1536]{2,0,1:T(8,128)} async-done(((f32[1024,1,1536]{2,0,1:T(8,128)}), f32[128,1,1536]{2,0,1:T(8,128)}) %reduce-scatter.12.cloned.1.call-update) | async-done | bytes 786448 | tf_op jit(solution)/shard_map/reduce_scatter | solution.py:343
  291.2 295.6 %all-reduce.9 = (bf16[1,128,1536]{2,0,1:T(2,128)(2,1)S(1)}, bf16[1,4608]{1,0:T(2,128)(2,1)S(1)}, bf16[768]{0:T(1024)(128)(2,1)}) all-reduce(f32[1,128,1536]{2,0,1:T(1,128)S(1)} %pad_maximum_fusion, f32[1,4608]{1,0:T(1,128)S(1)} %constant_dynamic-update-slice_fusion.1, ...), channel_id=4, replica_groups=mesh['band'=4,'seq'=8] {'seq'}, use_global_device_ids=true, to_apply=%region_25.26.clone | all-reduce | flops 201984 | bytes 1211904
  598.0 5.2 fusion.136
  604.4 5.1 fusion.165
  616.0 70.5 %reduce-scatter.14.cloned.1.call-done = f32[768,96]{0,1:T(8,128)} async-done(((f32[768,768]{0,1:T(8,128)}), f32[768,96]{0,1:T(8,128)}) %reduce-scatter.14.cloned.1.call-update) | async-done | bytes 294928 | tf_op jit(solution)/shard_map/reduce_scatter | solution.py:389
  688.1 5.0 convolution_reduce_fusion.2
  695.1 63.6 %reduce-scatter.26.cloned.1.call-done = f32[768,96]{0,1:T(8,128)} async-done(((f32[768,768]{0,1:T(8,128)}), f32[768,96]{0,1:T(8,128)}) %reduce-scatter.26.cloned.1.call-update) | async-done | bytes 294928 | tf_op jit(solution)/shard_map/reduce_scatter | solution.py:396
  760.4 70.7 %reduce-scatter.24.cloned.1.call-done = f32[768,96]{0,1:T(8,128)} async-done(((f32[768,768]{0,1:T(8,128)}), f32[768,96]{0,1:T(8,128)}) %reduce-scatter.24.cloned.1.call-update) | async-done | bytes 294928 | tf_op jit(solution)/shard_map/reduce_scatter | solution.py:395
  832.7 70.9 %reduce-scatter.18.cloned.1.call-done = f32[768,96]{0,1:T(8,128)} async-done(((f32[768,768]{0,1:T(8,128)}), f32[768,96]{0,1:T(8,128)}) %reduce-scatter.18.cloned.1.call-update) | async-done | bytes 294928 | tf_op jit(solution)/shard_map/reduce_scatter | solution.py:391
  905.2 70.5 %reduce-scatter.16.cloned.1.call-done = f32[768,96]{0,1:T(8,128)} async-done(((f32[768,768]{0,1:T(8,128)}), f32[768,96]{0,1:T(8,128)}) %reduce-scatter.16.cloned.1.call-update) | async-done | bytes 294928 | tf_op jit(solution)/shard_map/reduce_scatter | solution.py:390
  977.4 163.3 %reduce-scatter.32.cloned.1.call-done = f32[3072,96]{0,1:T(8,128)} async-done(((f32[3072,768]{0,1:T(8,128)}), f32[3072,96]{0,1:T(8,128)}) %reduce-scatter.32.cloned.1.call-update) | async-done | bytes 1179664 | tf_op jit(solution)/shard_map/reduce_scatter | solution.py:399
  1142.9 162.5 %reduce-scatter.30.cloned.1.call-done = f32[768,384]{1,0:T(8,128)} async-done(((f32[768,3072]{1,0:T(8,128)}), f32[768,384]{1,0:T(8,128)}) %reduce-scatter.30.cloned.1.call-update) | async-done | bytes 1179664 | tf_op jit(solution)/shard_map/reduce_scatter | solution.py:398
  1312.3 15.0 %all-reduce.3 = (bf16[256,96]{0,1:T(8,128)(2,1)}, bf16[96]{0:T(256)(128)(2,1)}) all-reduce(bf16[256,96]{0,1:T(8,128)(2,1)} %multiply_convert_fusion.5, bf16[96]{0:T(256)(128)(2,1)} %dynamic-slice.21), channel_id=1, replica_groups=mesh['band'=4,'seq'=8] {'band'}, use_global_device_ids=true, to_apply=%region_33.34 | all-reduce | flops 24672 | bytes 98688 | tf_op jit(solution)/shard_map/psum | solution.py:407
  1335.1 47.8 %all-reduce.8.cloned.1.call-done = (bf16[768,96]{0,1:T(8,128)(2,1)}, bf16[768,576]{0,1:T(8,128)(2,1)}, bf16[768,96]{0,1:T(8,128)(2,1)}, bf16[768,96]{0,1:T(8,128...) async-done(((bf16[768,96]{0,1:T(8,128)(2,1)}, ...) | async-done | bytes 3391504 | tf_op jit(solution)/shard_map/psum | solution.py:407
  (437 shorter events, 182.0 us)
Async XLA Ops:
  7.2 96.2 %copy-start = (bf16[768,768]{1,0:T(8,128)(2,1)S(1)}, bf16[768,768]{1,0:T(8,128)(2,1)}, u32[]{:S(2)}) copy-start(bf16[768,768]{1,0:T(8,128)(2,1)} %param.38) | copy-start | bytes 3538948
  7.2 77.2 %all-gather.3.cloned.1.call-start = ((), (), s32[]{:S(2)}) async-start(), calls=%async_computation.22 | async-start | bytes 3538944 | tf_op jit(solution)/shard_map/all_gather | solution.py:204
  21.5 264.4 %reduce-scatter.12.cloned.1.call-start = ((), (), s32[]{:S(2)}) async-start(), calls=%async_computation.11 | async-start | bytes 7077888 | tf_op jit(solution)/shard_map/reduce_scatter | solution.py:343
  28.4 77.6 %copy-start.31 = (bf16[128,768]{0,1:T(8,128)(2,1)}, bf16[128,768]{0,1:T(8,128)(2,1)S(1)}, u32[]{:S(2)}) copy-start(bf16[128,768]{0,1:T(8,128)(2,1)S(1)} %copy.110) | copy-start | bytes 589828
  30.3 77.0 %copy-start.27 = (bf16[128,768]{0,1:T(8,128)(2,1)}, bf16[128,768]{0,1:T(8,128)(2,1)S(1)}, u32[]{:S(2)}) copy-start(bf16[128,768]{0,1:T(8,128)(2,1)S(1)} %copy.109) | copy-start | bytes 589828
  105.2 25.3 %copy-start.6 = (f32[1,128,768]{2,1,0:T(8,128)}, f32[1,128,768]{2,1,0:T(8,128)S(1)}, u32[]{:S(2)}) copy-start(f32[1,128,768]{2,1,0:T(8,128)S(1)} %get-tuple-element.417) | copy-start | bytes 1179652
  169.1 441.2 %reduce-scatter.22.cloned.1.call-start = ((), (), s32[]{:S(2)}) async-start(), calls=%async_computation.16 | async-start | bytes 2654208 | tf_op jit(solution)/shard_map/reduce_scatter | solution.py:394
  172.1 439.8 %reduce-scatter.28.cloned.1.call-start = ((), (), s32[]{:S(2)}) async-start(), calls=%async_computation.19 | async-start | bytes 2654208 | tf_op jit(solution)/shard_map/reduce_scatter | solution.py:397
  175.1 439.2 %reduce-scatter.20.cloned.1.call-start = ((), (), s32[]{:S(2)}) async-start(), calls=%async_computation.15 | async-start | bytes 2654208 | tf_op jit(solution)/shard_map/reduce_scatter | solution.py:392
  179.0 507.4 %reduce-scatter.14.cloned.1.call-start = ((), (), s32[]{:S(2)}) async-start(), calls=%async_computation.12 | async-start | bytes 2654208 | tf_op jit(solution)/shard_map/reduce_scatter | solution.py:389
  179.6 26.5 %copy-start.56 = (f32[768]{0:T(1024)S(1)}, f32[768]{0:T(1024)}, u32[]{:S(2)}) copy-start(f32[768]{0:T(1024)} %copy-done.55) | copy-start | bytes 9220
  179.6 26.5 %copy-start.70 = (f32[768]{0:T(1024)S(1)}, f32[768]{0:T(1024)}, u32[]{:S(2)}) copy-start(f32[768]{0:T(1024)} %copy-done.69) | copy-start | bytes 9220
  208.8 549.9 %reduce-scatter.26.cloned.1.call-start = ((), (), s32[]{:S(2)}) async-start(), calls=%async_computation.18 | async-start | bytes 2654208 | tf_op jit(solution)/shard_map/reduce_scatter | solution.py:396
  213.5 75.5 %copy-start.78 = (f32[128]{0:T(128)S(1)}, f32[128]{0:T(128)}, u32[]{:S(2)}) copy-start(f32[128]{0:T(128)} %copy-done.77) | copy-start | bytes 1540
  213.5 75.5 %copy-start.88 = (f32[128]{0:T(128)S(1)}, f32[128]{0:T(128)}, u32[]{:S(2)}) copy-start(f32[128]{0:T(128)} %copy-done.87) | copy-start | bytes 1540
  589.7 241.4 %reduce-scatter.24.cloned.1.call-start = ((), (), s32[]{:S(2)}) async-start(), calls=%async_computation.17 | async-start | bytes 2654208 | tf_op jit(solution)/shard_map/reduce_scatter | solution.py:395
  592.4 311.2 %reduce-scatter.18.cloned.1.call-start = ((), (), s32[]{:S(2)}) async-start(), calls=%async_computation.14 | async-start | bytes 2654208 | tf_op jit(solution)/shard_map/reduce_scatter | solution.py:391
  594.5 381.3 %reduce-scatter.16.cloned.1.call-start = ((), (), s32[]{:S(2)}) async-start(), calls=%async_computation.13 | async-start | bytes 2654208 | tf_op jit(solution)/shard_map/reduce_scatter | solution.py:390
  596.6 544.1 %reduce-scatter.32.cloned.1.call-start = ((), (), s32[]{:S(2)}) async-start(), calls=%async_computation.21 | async-start | bytes 10616832 | tf_op jit(solution)/shard_map/reduce_scatter | solution.py:399
  603.2 702.2 %reduce-scatter.30.cloned.1.call-start = ((), (), s32[]{:S(2)}) async-start(), calls=%async_computation.20 | async-start | bytes 10616832 | tf_op jit(solution)/shard_map/reduce_scatter | solution.py:398
  609.6 773.4 %all-reduce.8.cloned.1.call-start = ((), (), s32[]{:S(2)}) async-start(), calls=%async_computation.23 | async-start | bytes 6782976 | tf_op jit(solution)/shard_map/psum | solution.py:407
  1309.5 24.7 %copy-start.14 = (f32[1,128,768]{2,1,0:T(8,128)S(1)}, f32[1,128,768]{2,1,0:T(8,128)}, u32[]{:S(2)}) copy-start(f32[1,128,768]{2,1,0:T(8,128)} %copy-done.13) | copy-start | bytes 1179652
  1309.5 24.7 %copy-start.89 = (f32[128]{0:T(128)S(1)}, f32[128]{0:T(128)}, u32[]{:S(2)}) copy-start(f32[128]{0:T(128)} %copy-done.87) | copy-start | bytes 1540
  1309.5 24.7 %copy-start.103 = (pred[128]{0:T(512)(128)(4,1)S(1)}, pred[128]{0:T(512)(128)(4,1)}, u32[]{:S(2)}) copy-start(pred[128]{0:T(512)(128)(4,1)} %add_compare_fusion.3) | copy-start | bytes 388
  (101 other events, 408.1 us)
Sparse Core Ops, SparseCore 0:
  21.6 62.7 all-gather.2
  169.3 116.6 reduce-scatter.11
  289.5 113.1 reduce-scatter.21
  406.0 111.6 reduce-scatter.27
  521.0 93.2 reduce-scatter.19
  617.7 68.7 reduce-scatter.13
  689.9 68.7 reduce-scatter.25
  762.3 68.7 reduce-scatter.23
  834.6 68.9 reduce-scatter.17
  906.9 68.7 reduce-scatter.15
  979.4 161.3 reduce-scatter.31
  1144.1 161.2 reduce-scatter.29
  1310.4 72.5 all-reduce.7
where the time goes:
time: 1410 us; the launch traced here: 1400 us
  waiting for transfers between devices  846 us (60%)
  blocking collectives  311 us (22%)
  matrix products  112 us (8%)
  other arithmetic  67.3 us (5%)
  local copies, waits for them, and re-layouts  44.2 us (3%)
  between operations  18.4 us (1%)
    unnamed x1, blocking collectives  296 us
    reduce_scatter x1, waiting for transfers between devices, on_device(): lax.psum_scatter(grad_w_mlp_out, 'seq', scatter_dimension=1, tiled=True)  163 us
    reduce_scatter x1, waiting for transfers between devices, on_device(): lax.psum_scatter(grad_w_mlp_in, 'seq', scatter_dimension=1, tiled=True)  163 us
    reduce_scatter x1, waiting for transfers between devices, on_device(): lax.psum_scatter(blocks.reshape(rows * lax.axis_size('seq'), clips, 2 * w...  72.4 us
    reduce_scatter x1, waiting for transfers between devices, on_device(): lax.psum_scatter(grad_w_value, 'seq', scatter_dimension=1, tiled=True)  70.9 us
    reduce_scatter x1, waiting for transfers between devices, on_device(): lax.psum_scatter(grad_w_cross_key, 'seq', scatter_dimension=1, tiled=True)  70.7 us
    reduce_scatter x1, waiting for transfers between devices, on_device(): lax.psum_scatter(grad_w_key, 'seq', scatter_dimension=1, tiled=True)  70.5 us
    reduce_scatter x1, waiting for transfers between devices, on_device(): lax.psum_scatter(grad_w_query, 'seq', scatter_dimension=1, tiled=True)  70.5 us
  transfers between devices with their start and end apart: 13, of which 11 were waited for; matrix products, arithmetic and copies ran while one was open for 8% of the time, Pallas kernels for 0%

commit v1 on v0

--- a/solution.py
+++ b/solution.py
@@ -3,6 +3,8 @@
 import jax
 import jax.numpy as jnp
 from jax import lax
+from jax.experimental import pallas as pl
+from jax.experimental.pallas import tpu as pltpu
 from jax.sharding import PartitionSpec as P
 
 H = 12
@@ -132,6 +134,254 @@
 def own_columns(values, place, count):
     share = values.shape[1] // count
     return lax.dynamic_slice_in_dim(values, place * share, share, 1)
+
+
+MESH = pl.DeviceIdType.MESH
+D = 768
+PART = 48
+
+PRODUCTS = (
+    [(0, j) for j in range(4)]
+    + [(1 + j, 4) for j in range(4)]
+    + [(5, 5), (6, 6), (7, 7), (8, 8), (8, 9)]
+    + [(9, 10), (9, 11), (9, 12)]
+)
+LEFTS = 10
+RIGHTS = 13
+TEXT_UNIT = 8
+
+
+def places():
+    band, seq = lax.axis_index("band"), lax.axis_index("seq")
+    return lax.div(band, 2), lax.rem(band, 2), lax.div(seq, 2), lax.rem(seq, 2)
+
+
+def device(y, core, z, x):
+    return (y * 2 + core, z * 2 + x)
+
+
+def remote(src, dst, send, recv, target):
+    return pltpu.make_async_remote_copy(
+        src_ref=src, dst_ref=dst, send_sem=send, recv_sem=recv, device_id=target, device_id_type=MESH
+    )
+
+
+def weight_kernel(
+    left_ref,
+    right_ref,
+    small_ref,
+    mlp_in_ref,
+    mlp_out_ref,
+    gt,
+    grecv,
+    lrecv,
+    psend,
+    pown,
+    precv,
+    qsend,
+    qown,
+    qrecv,
+    rsend,
+    rown,
+    rrecv,
+    final,
+    ls,
+    lr,
+    gs,
+    gr,
+    ps,
+    pr,
+    qs,
+    qr,
+    rs,
+    rr,
+    fs,
+    fr,
+):
+    y, core, z, x = places()
+    other_x, other_core, other_y = 1 - x, 1 - core, 1 - y
+    partners = [
+        device(y, core, z, other_x),
+        device(y, other_core, z, x),
+        device(other_y, core, z, x),
+        device(other_y, other_core, z, x),
+    ] + [device(y, core, lax.rem(z + k, 4), x) for k in (1, 2, 3)]
+    barrier = pltpu.get_barrier_semaphore()
+    for partner in partners:
+        pl.semaphore_signal(barrier, inc=1, device_id=partner, device_id_type=MESH)
+    pl.semaphore_wait(barrier, len(partners))
+
+    def left_copy(u):
+        return remote(left_ref.at[u], lrecv.at[u], ls.at[u], lr.at[u], partners[0])
+
+    def right_copy(u):
+        return remote(gt.at[u, other_x], grecv.at[u], gs.at[u], gr.at[u], partners[0])
+
+    def core_copy(i):
+        return remote(psend.at[i], precv.at[i], ps.at[i], pr.at[i], partners[1])
+
+    def y_copy(i):
+        return remote(qsend.at[i], qrecv.at[i], qs.at[i], qr.at[i], partners[2])
+
+    def z_copy(i, k):
+        return remote(
+            rsend.at[i, lax.rem(z + k, 4)],
+            rrecv.at[i, k],
+            rs.at[i, k],
+            rr.at[i, k],
+            partners[3 + k],
+        )
+
+    def last_copy(i, j):
+        return remote(
+            final.at[i, core, y], final.at[i, core, y], fs.at[i, j], fr.at[i, j], partners[j]
+        )
+
+    for u in range(RIGHTS):
+        turned = jnp.transpose(right_ref[u].astype(jnp.float32)).astype(jnp.bfloat16)
+        for s in range(8):
+            for c in range(2):
+                at = s * 96 + c * PART
+                gt[u, s % 2, c, pl.ds((s // 2) * PART, PART), :] = turned[at : at + PART]
+        right_copy(u).start()
+        if u < LEFTS and u != TEXT_UNIT:
+            left_copy(u).start()
+
+    def stage_product(i):
+        left, right = PRODUCTS[i]
+        if i == 0 or PRODUCTS[i - 1][0] != left:
+            if left != TEXT_UNIT:
+                left_copy(left).wait_recv()
+        if i == 0 or PRODUCTS[i - 1][1] != right:
+            right_copy(right).wait_recv()
+        for c, keep in ((other_core, False), (core, True)):
+            mine, theirs = gt[right, x, c], grecv[right, c]
+            if left == TEXT_UNIT:
+                both = (mine.astype(jnp.float32) + theirs.astype(jnp.float32)).astype(jnp.bfloat16)
+                part = jnp.dot(both, left_ref[left], preferred_element_type=jnp.float32)
+            else:
+                part = jnp.dot(
+                    jnp.concatenate([mine, theirs], axis=1),
+                    jnp.concatenate([left_ref[left], lrecv[left]], axis=0),
+                    preferred_element_type=jnp.float32,
+                )
+            if keep:
+                pown[i % 2] = part
+            else:
+                psend[i] = part.astype(jnp.bfloat16)
+                core_copy(i).start()
+
+    def stage_core(i):
+        core_copy(i).wait_recv()
+        total = pown[i % 2] + precv[i].astype(jnp.float32)
+        for h in range(2):
+            half = total[:, h * 384 : (h + 1) * 384]
+
+            @pl.when(h == y)
+            def _():
+                qown[i % 2] = half
+
+            @pl.when(h != y)
+            def _():
+                qsend[i] = half.astype(jnp.bfloat16)
+
+        y_copy(i).start()
+
+    def stage_y(i):
+        y_copy(i).wait_recv()
+        total = qown[i % 2] + qrecv[i].astype(jnp.float32)
+        for k in range(4):
+            rsend[i, k] = total[k * PART : (k + 1) * PART].astype(jnp.bfloat16)
+            rown[i % 2, k] = total[k * PART : (k + 1) * PART]
+        for k in (1, 2, 3):
+            z_copy(i, k).start()
+
+    def stage_z(i):
+        for k in (1, 2, 3):
+            z_copy(i, k).wait_recv()
+        total = rown[i % 2, z]
+        for k in (1, 2, 3):
+            total = total + rrecv[i, k].astype(jnp.float32)
+        final[i, core, y] = total.astype(jnp.bfloat16)
+        for j in (1, 2, 3):
+            last_copy(i, j).start()
+
+    n = len(PRODUCTS)
+    stages = (stage_product, stage_core, stage_y, stage_z)
+    for step in range(n + 3):
+        for at, stage in reversed(list(enumerate(stages))):
+            if 0 <= step - at < n:
+                stage(step - at)
+
+    for i in range(n):
+        for j in (1, 2, 3):
+            last_copy(i, j).wait_recv()
+        whole = jnp.concatenate(
+            [jnp.concatenate([final[i, c, h] for h in range(2)], axis=1) for c in range(2)], axis=0
+        ).astype(jnp.float32)
+        turned = jnp.transpose(whole)
+        if i < 4:
+            mlp_in_ref[i] = turned
+        elif i < 8:
+            mlp_out_ref[pl.ds((i - 4) * D, D), :] = turned
+        else:
+            small_ref[i - 8] = turned
+    for u in range(LEFTS):
+        if u != TEXT_UNIT:
+            left_copy(u).wait_send()
+    for u in range(RIGHTS):
+        right_copy(u).wait_send()
+    for i in range(n):
+        core_copy(i).wait_send()
+        y_copy(i).wait_send()
+        for k in (1, 2, 3):
+            z_copy(i, k).wait_send()
+            last_copy(i, k).wait_send()
+
+
+def weight_sums(lefts, rights):
+    n = len(PRODUCTS)
+    dma = pltpu.SemaphoreType.DMA
+    return pl.pallas_call(
+        weight_kernel,
+        out_shape=(
+            jax.ShapeDtypeStruct((8, D, 96), jnp.float32),
+            jax.ShapeDtypeStruct((4, D, 96), jnp.float32),
+            jax.ShapeDtypeStruct((4 * D, 96), jnp.float32),
+        ),
+        in_specs=[pl.BlockSpec(memory_space=pltpu.VMEM)] * 2,
+        out_specs=(pl.BlockSpec(memory_space=pltpu.VMEM),) * 3,
+        scratch_shapes=[
+            pltpu.VMEM((RIGHTS, 2, 2, 192, 128), jnp.bfloat16),
+            pltpu.VMEM((RIGHTS, 2, 192, 128), jnp.bfloat16),
+            pltpu.VMEM((LEFTS, 128, D), jnp.bfloat16),
+            pltpu.VMEM((n, 192, D), jnp.bfloat16),
+            pltpu.VMEM((2, 192, D), jnp.float32),
+            pltpu.VMEM((n, 192, D), jnp.bfloat16),
+            pltpu.VMEM((n, 192, 384), jnp.bfloat16),
+            pltpu.VMEM((2, 192, 384), jnp.float32),
+            pltpu.VMEM((n, 192, 384), jnp.bfloat16),
+            pltpu.VMEM((n, 4, PART, 384), jnp.bfloat16),
+            pltpu.VMEM((2, 4, PART, 384), jnp.float32),
+            pltpu.VMEM((n, 4, PART, 384), jnp.bfloat16),
+            pltpu.VMEM((n, 2, 2, PART, 384), jnp.bfloat16),
+            dma((LEFTS,)),
+            dma((LEFTS,)),
+            dma((RIGHTS,)),
+            dma((RIGHTS,)),
+            dma((n,)),
+            dma((n,)),
+            dma((n,)),
+            dma((n,)),
+            dma((n, 4)),
+            dma((n, 4)),
+            dma((n, 4)),
+            dma((n, 4)),
+        ],
+        compiler_params=pltpu.CompilerParams(
+            collective_id=0, has_side_effects=True, vmem_limit_bytes=60 * 1024 * 1024
+        ),
+    )(lefts, rights)
 
 
 def on_device(
@@ -385,6 +635,338 @@
         (((0,), (0,)), ((), ())),
         precision=lax.Precision.HIGHEST,
     )
+    by_block = lambda values: jnp.transpose(
+        values.reshape(tokens, 8, 4, 96), (2, 0, 1, 3)
+    ).reshape(4, tokens, width)
+    lefts = jnp.concatenate(
+        [
+            flatten(mlp_in)[None],
+            jnp.transpose(activation.reshape(tokens, 4, width), (1, 0, 2)),
+            jnp.stack(
+                [flatten(cross_low), flatten(cross_in), flatten(attn_low), text_flat, attn_flat]
+            ),
+        ],
+        axis=0,
+    )
+    text_keys, text_values = [
+        narrow(values.reshape(clips * text_count, width))
+        for values in (cross_key_part, cross_value_part)
+    ]
+    rights = jnp.concatenate(
+        [
+            by_block(grad_pre),
+            jnp.stack(
+                [
+                    grad_mlp,
+                    grad_cross_out,
+                    grad_cross_query,
+                    grad_attn_proj,
+                    text_keys,
+                    text_values,
+                    grad_query,
+                    grad_key,
+                    grad_value,
+                ]
+            ),
+        ],
+        axis=0,
+    )
+    small, mlp_in_parts, sum_mlp_out = weight_sums(lefts, rights)
+    sum_mlp_in = jnp.transpose(mlp_in_parts, (1, 0, 2)).reshape(width, 4 * 96)
+    (
+        sum_cross_out,
+        sum_cross_query,
+        sum_attn_out,
+        sum_cross_key,
+        sum_cross_value,
+        sum_query,
+        sum_key,
+        sum_value,
+    ) = [small[i] for i in range(8)]
+    gain_share = width // seq_count
+    sum_gain = lax.dynamic_slice_in_dim(
+        lax.psum(grad_gain_part, ("band", "seq")), seq_place * gain_share, gain_share, 0
+    )
+    replicated = (
+        own_columns(grad_w_time_in, seq_place, seq_count),
+        own_columns(grad_w_time_out, seq_place, seq_count),
+        own_columns(grad_w_adaln, seq_place, seq_count),
+    )
+    sum_time_in, sum_time_out, sum_adaln = jax.tree.map(
+        lambda part: part.astype(jnp.float32), lax.psum(for_sending(replicated), "band")
+    )
+    return (
+        block_out,
+        grad_frames,
+        grad_text,
+        sum_time_in,
+        sum_time_out,
+        sum_adaln,
+        sum_query,
+        sum_key,
+        sum_value,
+        sum_attn_out,
+        sum_gain,
+        sum_cross_query,
+        sum_cross_key,
+        sum_cross_value,
+        sum_cross_out,
+        sum_mlp_in,
+        sum_mlp_out,
+    )
+
+
+def on_device_general(
+    frames,
+    text,
+    timesteps,
+    frame_lengths,
+    text_mask,
+    cotangent,
+    w_time_in,
+    w_time_out,
+    w_adaln,
+    w_query,
+    w_key,
+    w_value,
+    w_attn_out,
+    cross_gain,
+    w_cross_query,
+    w_cross_key,
+    w_cross_value,
+    w_cross_out,
+    w_mlp_in,
+    w_mlp_out,
+):
+    clips = frames.shape[0]
+    rows = frames.shape[1]
+    width = frames.shape[2]
+    tokens = clips * rows
+    text_count = text.shape[1]
+    seq_place = lax.axis_index("seq")
+    seq_count = lax.axis_size("seq")
+    offset = seq_place * rows
+    inputs = frames.astype(jnp.float32)
+    own_valid = (offset + jnp.arange(rows))[None, :] < frame_lengths[:, None]
+    row_valid = own_valid[:, :, None]
+    text_valid = text_mask != 0
+
+    def flatten(values):
+        return values.reshape(tokens, values.shape[-1])
+
+    def unflatten(values):
+        return values.reshape(clips, rows, values.shape[-1])
+
+    time_vector = narrow(time_embed(timesteps, w_time_in.shape[0]))
+    time_first = product(time_vector, w_time_in)
+    time_hidden = narrow(jax.nn.silu(time_first))
+    time_out = product(time_hidden, w_time_out)
+    condition = narrow(jax.nn.silu(time_out))
+    modulation = product(condition, w_adaln)
+    shift_attn, scale_attn, gate_attn, shift_mlp, scale_mlp, gate_mlp = [
+        piece[:, None, :] for piece in jnp.split(modulation, 6, axis=1)
+    ]
+    normed_attn, scaling_attn = layer_norm(inputs)
+    attn_in = narrow(normed_attn * (1.0 + scale_attn) + shift_attn)
+    attn_flat = flatten(attn_in)
+    query_flat = narrow(product(attn_flat, w_query))
+    queries = split_heads(unflatten(query_flat))
+    kv_local = unflatten(
+        jnp.concatenate(
+            [narrow(product(attn_flat, w_key)), narrow(product(attn_flat, w_value))], axis=1
+        )
+    )
+    start_state = (
+        jnp.full((clips, rows, H), -1e30, jnp.float32),
+        jnp.zeros((clips, rows, H), jnp.float32),
+        jnp.zeros((clips, rows, H, HD), jnp.float32),
+    )
+    row_max, row_sum, weighted = forward_piece(
+        start_state,
+        lax.all_gather(kv_local, "seq", axis=1, tiled=True),
+        jnp.int32(0),
+        queries,
+        frame_lengths,
+    )
+    attended = weighted / row_sum[..., None]
+    log_total = row_max + jnp.log(row_sum)
+    attn_low = narrow(attended.reshape(clips, rows, width))
+    attn_proj = unflatten(product(flatten(attn_low), w_attn_out))
+    middle = inputs + gate_attn * attn_proj
+    normed_cross, scaling_cross = layer_norm(middle)
+    gain_values = cross_gain.astype(jnp.float32)
+    cross_in = narrow(normed_cross * gain_values)
+    cross_queries = split_heads(unflatten(narrow(product(flatten(cross_in), w_cross_query))))
+    text_flat = text.reshape(clips * text_count, width)
+    cross_keys = split_heads(
+        narrow(product(text_flat, w_cross_key)).reshape(clips, text_count, width)
+    )
+    cross_values = split_heads(
+        narrow(product(text_flat, w_cross_value)).reshape(clips, text_count, width)
+    )
+    cross_scores = masked_scores(cross_queries, cross_keys, text_valid)
+    cross_max = jnp.max(cross_scores, axis=-1, keepdims=True)
+    cross_total = cross_max + jnp.log(
+        jnp.sum(jnp.exp(cross_scores - cross_max), axis=-1, keepdims=True)
+    )
+    cross_probs = jnp.exp(cross_scores - cross_total)
+    cross_probs_low = narrow(cross_probs)
+    cross_attended = jnp.einsum(
+        "cqhk,ckhd->cqhd", cross_probs_low, cross_values, preferred_element_type=jnp.float32
+    )
+    cross_low = narrow(cross_attended.reshape(clips, rows, width))
+    after_cross = middle + unflatten(product(flatten(cross_low), w_cross_out))
+    normed_mlp, scaling_mlp = layer_norm(after_cross)
+    mlp_in = narrow(normed_mlp * (1.0 + scale_mlp) + shift_mlp)
+    pre_act = product(flatten(mlp_in), w_mlp_in)
+    activation = narrow(jax.nn.gelu(pre_act, approximate=True))
+    mlp_out = unflatten(product(activation, w_mlp_out))
+    result = after_cross + gate_mlp * mlp_out
+    block_out = jnp.where(row_valid, result, inputs).astype(jnp.bfloat16)
+    grad_out = cotangent.astype(jnp.float32)
+    grad_res = jnp.where(row_valid, grad_out, 0.0)
+    grad_mlp = flatten(narrow(gate_mlp * grad_res))
+    grad_w_mlp_out = transposed_left(activation, grad_mlp)
+    grad_act = transposed_right(grad_mlp, w_mlp_out)
+    gelu_pull = jax.vjp(lambda values: jax.nn.gelu(values, approximate=True), pre_act)[1]
+    grad_pre = narrow(gelu_pull(grad_act)[0])
+    grad_w_mlp_in = transposed_left(flatten(mlp_in), grad_pre)
+    grad_mlp_in = unflatten(transposed_right(grad_pre, w_mlp_in))
+    grad_after = grad_res + norm_back(normed_mlp, scaling_mlp, grad_mlp_in * (1.0 + scale_mlp))
+    grad_cross_out = flatten(narrow(grad_after))
+    grad_w_cross_out = transposed_left(flatten(cross_low), grad_cross_out)
+    grad_cross_attn = split_heads(unflatten(narrow(transposed_right(grad_cross_out, w_cross_out))))
+    cross_delta = jnp.sum(grad_cross_attn.astype(jnp.float32) * cross_attended, axis=-1)
+    cross_grad_probs = jnp.einsum(
+        "cqhd,ckhd->cqhk", grad_cross_attn, cross_values, preferred_element_type=jnp.float32
+    )
+    cross_grad_scores = narrow(cross_probs * (cross_grad_probs - cross_delta[..., None]))
+    grad_cross_query = narrow(
+        jnp.einsum(
+            "cqhk,ckhd->cqhd", cross_grad_scores, cross_keys, preferred_element_type=jnp.float32
+        )
+        * 0.125
+    ).reshape(tokens, width)
+    cross_key_part = (
+        jnp.einsum(
+            "cqhk,cqhd->ckhd", cross_grad_scores, cross_queries, preferred_element_type=jnp.float32
+        )
+        * 0.125
+    )
+    cross_value_part = jnp.einsum(
+        "cqhk,cqhd->ckhd", cross_probs_low, grad_cross_attn, preferred_element_type=jnp.float32
+    )
+    cross_kv_part = jnp.concatenate(
+        [
+            cross_key_part.reshape(clips, text_count, width),
+            cross_value_part.reshape(clips, text_count, width),
+        ],
+        axis=2,
+    )
+    text_total = lax.psum_scatter(cross_kv_part, "seq", scatter_dimension=1, tiled=True)
+    text_share = text_total.shape[1]
+    grad_cross_key = narrow(text_total[:, :, :width]).reshape(clips * text_share, width)
+    grad_cross_value = narrow(text_total[:, :, width:]).reshape(clips * text_share, width)
+    text_own = lax.dynamic_slice_in_dim(text, seq_place * text_share, text_share, 1).reshape(
+        clips * text_share, width
+    )
+    grad_text = (
+        transposed_right(grad_cross_key, w_cross_key)
+        + transposed_right(grad_cross_value, w_cross_value)
+    ).reshape(clips, text_share, width)
+    grad_w_cross_key = transposed_left(text_own, grad_cross_key)
+    grad_w_cross_value = transposed_left(text_own, grad_cross_value)
+    grad_w_cross_query = transposed_left(flatten(cross_in), grad_cross_query)
+    grad_cross_in = unflatten(transposed_right(grad_cross_query, w_cross_query))
+    grad_gain_part = jnp.sum(grad_cross_in * normed_cross, axis=(0, 1))
+    grad_mid = grad_after + norm_back(normed_cross, scaling_cross, grad_cross_in * gain_values)
+    grad_attn_proj = flatten(narrow(gate_attn * grad_mid))
+    grad_w_attn_out = transposed_left(flatten(attn_low), grad_attn_proj)
+    grad_attn_flat = narrow(transposed_right(grad_attn_proj, w_attn_out))
+    grad_heads = split_heads(unflatten(grad_attn_flat))
+    row_delta = jnp.sum(grad_heads.astype(jnp.float32) * attended, axis=-1)
+    zero_heads = jnp.zeros((clips, rows, H, HD), jnp.float32)
+    gathered = lax.all_gather(kv_local, "seq", axis=1, tiled=True)
+    query_grad = query_piece(
+        zero_heads, gathered, 0, queries, grad_heads, log_total, row_delta, frame_lengths
+    )
+    anchor = jnp.int32(0)
+    block_size = math.gcd(rows * lax.axis_size("seq"), key_block)
+
+    def key_one_block(counter):
+        rows_in = lax.dynamic_slice_in_dim(gathered, counter * block_size, block_size, 1)
+        key_valid = block_valid(anchor, counter * block_size, block_size, frame_lengths)
+        scores = masked_scores(queries, split_heads(rows_in[:, :, :width]), key_valid)
+        attn_probs = jnp.exp(scores - log_total[..., None])
+        grad_probs = jnp.einsum(
+            "cqhd,ckhd->cqhk",
+            grad_heads,
+            split_heads(rows_in[:, :, width:]),
+            preferred_element_type=jnp.float32,
+        )
+        grad_scores = narrow(attn_probs * (grad_probs - row_delta[..., None]))
+        grad_keys = (
+            jnp.einsum("cqhk,cqhd->ckhd", grad_scores, queries, preferred_element_type=jnp.float32)
+            * 0.125
+        )
+        grad_values = jnp.einsum(
+            "cqhk,cqhd->ckhd", narrow(attn_probs), grad_heads, preferred_element_type=jnp.float32
+        )
+        joined = jnp.concatenate(
+            [
+                grad_keys.reshape(clips, block_size, width),
+                grad_values.reshape(clips, block_size, width),
+            ],
+            axis=2,
+        )
+        return jnp.transpose(joined, (1, 0, 2))
+
+    blocks = lax.map(key_one_block, jnp.arange(rows * lax.axis_size("seq") // block_size))
+    kv_term = lax.psum_scatter(
+        blocks.reshape(rows * lax.axis_size("seq"), clips, 2 * width),
+        "seq",
+        scatter_dimension=0,
+        tiled=True,
+    )
+    kv_grad = jnp.transpose(kv_term, (1, 0, 2))
+    grad_query = narrow(query_grad.reshape(tokens, width))
+    grad_key = flatten(narrow(kv_grad[:, :, :width]))
+    grad_value = flatten(narrow(kv_grad[:, :, width:]))
+    grad_w_query = transposed_left(attn_flat, grad_query)
+    grad_w_key = transposed_left(attn_flat, grad_key)
+    grad_w_value = transposed_left(attn_flat, grad_value)
+    grad_attn_in = unflatten(
+        transposed_right(grad_query, w_query)
+        + transposed_right(grad_key, w_key)
+        + transposed_right(grad_value, w_value)
+    )
+    grad_inputs = grad_mid + norm_back(normed_attn, scaling_attn, grad_attn_in * (1.0 + scale_attn))
+    grad_frames = jnp.where(row_valid, grad_inputs, grad_out).astype(jnp.bfloat16)
+    modulation_part = jnp.concatenate(
+        [
+            jnp.sum(grad_attn_in, axis=1),
+            jnp.sum(grad_attn_in * normed_attn, axis=1),
+            jnp.sum(grad_mid * attn_proj, axis=1),
+            jnp.sum(grad_mlp_in, axis=1),
+            jnp.sum(grad_mlp_in * normed_mlp, axis=1),
+            jnp.sum(grad_res * mlp_out, axis=1),
+        ],
+        axis=1,
+    )
+    modulation_total = lax.psum(modulation_part, "seq")
+    grad_modulation = narrow(modulation_total)
+    grad_w_adaln = transposed_left(condition, grad_modulation)
+    grad_condition = transposed_right(grad_modulation, w_adaln)
+    grad_time_out = narrow(jax.vjp(jax.nn.silu, time_out)[1](grad_condition)[0])
+    grad_w_time_out = transposed_left(time_hidden, grad_time_out)
+    grad_time_hidden = transposed_right(grad_time_out, w_time_out)
+    grad_time_first = jax.vjp(jax.nn.silu, time_first)[1](grad_time_hidden)[0]
+    grad_w_time_in = lax.dot_general(
+        time_vector.astype(jnp.float32),
+        grad_time_first,
+        (((0,), (0,)), ((), ())),
+        precision=lax.Precision.HIGHEST,
+    )
     shared = (
         lax.psum_scatter(grad_w_query, "seq", scatter_dimension=1, tiled=True),
         lax.psum_scatter(grad_w_key, "seq", scatter_dimension=1, tiled=True),
@@ -466,8 +1048,9 @@
         P(),
         P(),
     )
+    paired = mesh.shape["band"] == 4 and mesh.shape["seq"] == 8
     return jax.shard_map(
-        on_device,
+        on_device if paired else on_device_general,
         mesh=mesh,
         in_specs=placed,
         out_specs=(

time: 1410 us -> 747 us (0.53)
  waiting for transfers between devices: 846 us -> 92.4 us
  Pallas kernels: 0 us -> 118 us
  local copies, waits for them, and re-layouts: 44.2 us -> 87.9 us
  matrix products: 112 us -> 77.3 us
  other arithmetic: 67.3 us -> 37.8 us
    reduce_scatter x10 -> x0, waiting for transfers between devices: 673 us -> none  [the longest x1 163 us: on_device(): lax.psum_scatter(grad_w_mlp_out, 'seq', scatter_dimension=1, tiled=True)]
    unnamed x1 -> x0, blocking collectives: 296 us -> none
    psum x1 -> x3, blocking collectives: 15 us -> 305 us  [the longest x1 253 us: on_device(): modulation_total = lax.psum(modulation_part, 'seq')]
    pallas_call x0 -> x1, Pallas kernels: none -> 118 us  [weight_sums(): pl.pallas_call(weight_kernel, out_shape=(jax.ShapeDtypeStruct((8, D, 96),...]
    psum x1, waiting for transfers between devices: 47.8 us -> 4.78 us  [on_device(): lax.psum(for_sending(replicated), 'band')]
    reduce_scatter x1, waiting for transfers between devices: 72.4 us -> 31.3 us  [on_device(): lax.psum_scatter(blocks.reshape(rows * lax.axis_size('seq'), clips, 2 * w...]
    dot_general x10 -> x0, matrix products: 29.5 us -> none  [transposed_left(): lax.dot_general(left, right, (((0,), (0,)), ((), ())), preferred_element_...]
    unnamed x229 -> x232, local copies, waits for them, and re-layouts: 13.8 us -> 35.7 us
  transfers between devices with their start and end apart: 13 -> 3, of which waited for: 11 -> 3; matrix products, arithmetic and copies ran while one was open for 8% -> 9% of each run, Pallas kernels for 0% -> 0%
where the time goes in v1:
time: 747 us; the launch traced here: 740 us
  blocking collectives  305 us (41%)
  Pallas kernels  118 us (16%)
  waiting for transfers between devices  92.4 us (12%)
  local copies, waits for them, and re-layouts  87.9 us (12%)
  matrix products  77.3 us (10%)
  other arithmetic  37.8 us (5%)
  between operations  17.4 us (2%)
    psum x1, blocking collectives, on_device(): modulation_total = lax.psum(modulation_part, 'seq')  253 us
    pallas_call x1, Pallas kernels, weight_sums(): pl.pallas_call(weight_kernel, out_shape=(jax.ShapeDtypeStruct((8, D, 96),...  118 us
    all_gather x1, waiting for transfers between devices, on_device(): lax.all_gather(kv_local, 'seq', axis=1, tiled=True)  56.2 us
    psum x1, blocking collectives, on_device(): lax.psum(grad_gain_part, ('band', 'seq'))  40.6 us
    unnamed x232, local copies, waits for them, and re-layouts  35.7 us
    reduce_scatter x1, waiting for transfers between devices, on_device(): lax.psum_scatter(blocks.reshape(rows * lax.axis_size('seq'), clips, 2 * w...  31.3 us
    dot_general x13, matrix products, product(): return jnp.dot(left, right, preferred_element_type=jnp.float32)  22.5 us
    dot_general x12, matrix products, transposed_right(): lax.dot_general(left, right, (((1,), (1,)), ((), ())), preferred_element_...  18.2 us
  transfers between devices with their start and end apart: 3, of which 3 were waited for; matrix products, arithmetic and copies ran while one was open for 9% of the time, Pallas kernels for 0%

profile of v1, /device:TPU:0, one launch (start us, length us, event | category | flops | bytes accessed | tf_op | source)
XLA Modules:
  0.0 740.4 jit_solution(16672125097733598888)
XLA Ops:
  14.9 4.2 fusion.166
  28.1 56.2 %all-gather.3.cloned.1.call-done = bf16[1024,1536]{1,0:T(8,128)(2,1)} async-done(((bf16[128,1536]{1,0:T(8,128)(2,1)}), bf16[1024,1536]{1,0:T(8,128)(2,1)}) %all-gather.3.cloned.1.call-update) | async-done | bytes 3145744 | tf_op jit(solution)/shard_map/all_gather | solution.py:454
  84.3 4.7 copy.168
  89.0 12.6 %while.37 = (s32[]{:T(128)}, f32[1,128,12]{1,2,0:T(8,128)S(1)}, f32[1,128,12]{1,2,0:T(8,128)S(1)}, f32[1,128,12,64]{1,3,2,0:T(8,128)}, s32[2]{0:T(128)S(1)}, /*i...) while((s32[]{:T(128)}, f32[1,128,12]{1,2,0:T(8,128)S(1)}, ...), condition=%wide.region_5.6_spmd.clone, body=%wide.region_2.5_spmd.clone.sunk | while | flops 210282496 | bytes 18385184 | solution.py:99
  108.7 5.1 multiply_convert_fusion.1
  151.7 33.3 %while.36 = (s32[]{:T(128)}, f32[2,512,1,1536]{3,1,0,2:T(8,128)}, s32[2]{0:T(128)S(1)}, s32[1]{0:T(128)}, bf16[1,1024,1536]{1,2,0:T(8,128)(2,1)}, /*index=5*/bf1...) while((s32[]{:T(128)}, f32[2,512,1,1536]{3,1,0,2:T(8,128)}, ...), condition=%wide.region_21.22_spmd, body=%wide.region_20.21_spmd.sunk | while | flops 411698176 | bytes 43273988 | solution.py:592
  157.0 3.9 fusion.255
  173.4 3.9 fusion.255
  194.2 3.0 copy.182
  197.3 24.0 %while.38 = (s32[]{:T(128)}, f32[1,128,12,64]{1,3,2,0:T(8,128)}, s32[2]{0:T(128)S(1)}, bf16[1,1024,1536]{1,2,0:T(8,128)(2,1)S(1)}, s32[1]{0:T(128)}, /*index=5*/...) while((s32[]{:T(128)}, f32[1,128,12,64]{1,3,2,0:T(8,128)}, ...), condition=%wide.region_19.20_spmd.clone, body=%wide.region_18.19_spmd.clone.sunk | while | flops 307004416 | bytes 12989677 | solution.py:130
  201.0 3.5 fusion.268
  204.5 4.7 fusion.269
  212.9 3.5 fusion.268
  216.4 4.8 fusion.269
  222.6 40.6 %psum.39 = f32[768]{0:T(1024)S(1)} all-reduce(f32[768]{0:T(1024)S(1)} %copy-done.74), channel_id=1, replica_groups=mesh['band'=4,'seq'=8] {'band','seq'}, use_global_device_ids=true, to_apply=%region_37.38 | all-reduce | flops 768 | bytes 6144 | tf_op jit(solution)/shard_map/psum | solution.py:688
  271.4 31.3 %reduce-scatter.2.cloned.1.call-done = f32[128,1,1536]{2,0,1:T(8,128)} async-done(((f32[1024,1,1536]{2,0,1:T(8,128)}), f32[128,1,1536]{2,0,1:T(8,128)}) %reduce-scatter.2.cloned.1.call-update) | async-done | bytes 786448 | tf_op jit(solution)/shard_map/reduce_scatter | solution.py:593
  305.5 4.2 fusion.103
  309.8 252.9 %all-reduce.7 = (bf16[1,4608]{1,0:T(2,128)(2,1)S(1)}, bf16[1,128,1536]{2,0,1:T(2,128)(2,1)}) all-reduce(f32[1,4608]{1,0:T(1,128)S(1)} %constant_dynamic-update-slice_fusion.1, f32[1,128,1536]{2,0,1:T(1,128)S(1)} %copy-done.26), channel_id=1, replica_groups=mesh['band'=4,'seq'=8] {'seq'}, use_global_device_ids=true, to_apply=%region_32.33 | all-reduce | flops 201216 | bytes 1207296 | tf_op jit(solution)/shard_map/psum | solution.py:624
  562.6 5.0 convolution_reduce_fusion.2
  569.8 117.8 %shard_map.323 = (f32[8,768,96]{2,1,0:T(8,128)}, f32[4,768,96]{2,1,0:T(8,128)}, f32[3072,96]{1,0:T(8,128)}) custom-call(bf16[10,128,768]{2,1,0:T(8,128)(2,1)} %constant_dynamic-update-slice_fusion.7.left_ref, bf16[13,128,768]{2,1,0:T(8,128)(2,1)} %slice_dynamic-update-slice_fusion.right_ref), custom_call_target="tpu_custom_call" | custom-call | tf_op jit(solution)/shard_map/pallas_call | solution.py:345
  687.6 3.0 slice_bitcast_fusion
  694.2 11.4 %psum.36 = bf16[256,96]{0,1:T(8,128)(2,1)S(1)} all-reduce(bf16[256,96]{0,1:T(8,128)(2,1)S(1)} %multiply_convert_fusion.5), channel_id=1, replica_groups=mesh['band'=4,'seq'=8] {'band'}, use_global_device_ids=true, to_apply=%region_33.34 | all-reduce | flops 24576 | bytes 98304 | tf_op jit(solution)/shard_map/psum | solution.py:696
  718.6 3.0 copy.205
  724.7 4.8 all-reduce.6.cloned.1.call-done
  (405 shorter events, 146.7 us)
Async XLA Ops:
  7.2 95.6 %copy-start = (bf16[768,768]{1,0:T(8,128)(2,1)S(1)}, bf16[768,768]{1,0:T(8,128)(2,1)}, u32[]{:S(2)}) copy-start(bf16[768,768]{1,0:T(8,128)(2,1)} %param.38) | copy-start | bytes 3538948
  7.2 77.1 %all-gather.3.cloned.1.call-start = ((), (), s32[]{:S(2)}) async-start(), calls=%async_computation.2 | async-start | bytes 3538944 | tf_op jit(solution)/shard_map/all_gather | solution.py:454
  9.0 13.7 %copy-start.81 = (f32[128]{0:T(128)}, f32[128]{0:T(128)S(1)}, u32[]{:S(2)}) copy-start(f32[128]{0:T(128)S(1)} %broadcast_multiply_fusion.8) | copy-start | bytes 1540
  10.2 12.6 %copy-start.86 = (f32[128]{0:T(128)}, f32[128]{0:T(128)S(1)}, u32[]{:S(2)}) copy-start(f32[128]{0:T(128)S(1)} %add_rsqrt_fusion.2) | copy-start | bytes 1540
  21.4 281.4 %reduce-scatter.2.cloned.1.call-start = ((), (), s32[]{:S(2)}) async-start(), calls=%async_computation.1 | async-start | bytes 7077888 | tf_op jit(solution)/shard_map/reduce_scatter | solution.py:593
  25.1 80.5 %copy-start.32 = (bf16[128,768]{0,1:T(8,128)(2,1)}, bf16[128,768]{0,1:T(8,128)(2,1)S(1)}, u32[]{:S(2)}) copy-start(bf16[128,768]{0,1:T(8,128)(2,1)S(1)} %copy.170) | copy-start | bytes 589828
  89.0 13.8 %copy-start.63 = (f32[768]{0:T(1024)S(1)}, f32[768]{0:T(1024)}, u32[]{:S(2)}) copy-start(f32[768]{0:T(1024)} %get-tuple-element.409) | copy-start | bytes 9220
  106.7 34.7 %copy-start.4 = (f32[1,128,12,128]{1,3,2,0:T(8,128)}, f32[1,128,12,128]{1,3,2,0:T(8,128)S(1)}, u32[]{:S(2)}) copy-start(f32[1,128,12,128]{1,3,2,0:T(8,128)S(1)} %get-tuple-element.505) | copy-start | bytes 2359300
  108.4 21.1 %copy-start.6 = (f32[1,128,768]{2,1,0:T(8,128)}, f32[1,128,768]{2,1,0:T(8,128)S(1)}, u32[]{:S(2)}) copy-start(f32[1,128,768]{2,1,0:T(8,128)S(1)} %get-tuple-element.509) | copy-start | bytes 1179652
  108.4 7.4 %copy-start.93 = (f32[128]{0:T(128)}, f32[128]{0:T(128)S(1)}, u32[]{:S(2)}) copy-start(f32[128]{0:T(128)S(1)} %broadcast_multiply_fusion.6) | copy-start | bytes 1540
  108.7 8.1 %slice-start.2 = ((s8[4718592]{0:T(1024)(128)(4,1)}), s8[4194304]{0:T(1024)(128)(4,1)S(1)}, s32[]{:S(2)}) async-start(s8[4718592]{0:T(1024)(128)(4,1)} %bitcast.601), calls=%async_computation.6 | async-start | bytes 8388608
  119.0 7.6 %copy-start.23 = (f32[128,768]{1,0:T(8,128)}, f32[128,768]{1,0:T(8,128)S(1)}, u32[]{:S(2)}) copy-start(f32[128,768]{1,0:T(8,128)S(1)} %get-tuple-element.512) | copy-start | bytes 1179652
  185.1 544.4 %all-reduce.6.cloned.1.call-start = ((), (), s32[]{:S(2)}) async-start(), calls=%async_computation.3 | async-start | bytes 2064384 | tf_op jit(solution)/shard_map/psum | solution.py:696
  197.3 25.3 %copy-start.74 = (f32[768]{0:T(1024)S(1)}, f32[768]{0:T(1024)}, u32[]{:S(2)}) copy-start(f32[768]{0:T(1024)} %get-tuple-element.395) | copy-start | bytes 9220
  221.3 47.4 %copy-start.52 = (bf16[1,128,768]{2,1,0:T(8,128)(2,1)S(1)}, bf16[1,128,768]{2,1,0:T(8,128)(2,1)}, u32[]{:S(2)}) copy-start(bf16[1,128,768]{2,1,0:T(8,128)(2,1)} %copy.191) | copy-start | bytes 589828
  221.3 48.8 %copy-start.9 = (bf16[1,128,768]{2,1,0:T(8,128)(2,1)S(1)}, bf16[1,128,768]{2,1,0:T(8,128)(2,1)}, u32[]{:S(2)}) copy-start(bf16[1,128,768]{2,1,0:T(8,128)(2,1)} %param.26) | copy-start | bytes 589828
  221.3 48.8 %copy-start.60 = (f32[768]{0:T(1024)S(1)}, f32[768]{0:T(1024)}, u32[]{:S(2)}) copy-start(f32[768]{0:T(1024)} %copy-done.59) | copy-start | bytes 9220
  221.3 48.8 %copy-start.76 = (f32[768]{0:T(1024)S(1)}, f32[768]{0:T(1024)}, u32[]{:S(2)}) copy-start(f32[768]{0:T(1024)} %copy-done.75) | copy-start | bytes 9220
  221.3 48.8 %copy-start.82 = (f32[128]{0:T(128)S(1)}, f32[128]{0:T(128)}, u32[]{:S(2)}) copy-start(f32[128]{0:T(128)} %copy-done.81) | copy-start | bytes 1540
  221.3 48.8 %copy-start.87 = (f32[128]{0:T(128)S(1)}, f32[128]{0:T(128)}, u32[]{:S(2)}) copy-start(f32[128]{0:T(128)} %copy-done.86) | copy-start | bytes 1540
  221.3 49.6 %copy-start.46 = (bf16[768,768]{1,0:T(8,128)(2,1)S(1)}, bf16[768,768]{1,0:T(8,128)(2,1)}, u32[]{:S(2)}) copy-start(bf16[768,768]{1,0:T(8,128)(2,1)} %param.35) | copy-start | bytes 3538948
  269.3 34.6 %copy-start.48 = (bf16[768,768]{1,0:T(8,128)(2,1)S(1)}, bf16[768,768]{1,0:T(8,128)(2,1)}, u32[]{:S(2)}) copy-start(bf16[768,768]{1,0:T(8,128)(2,1)} %param.36) | copy-start | bytes 3538948
  271.4 33.1 %copy-start.50 = (bf16[768,768]{1,0:T(8,128)(2,1)S(1)}, bf16[768,768]{1,0:T(8,128)(2,1)}, u32[]{:S(2)}) copy-start(bf16[768,768]{1,0:T(8,128)(2,1)} %param.37) | copy-start | bytes 3538948
  721.6 12.0 %copy-start.1 = (bf16[768,768]{1,0:T(8,128)(2,1)S(1)}, bf16[768,768]{1,0:T(8,128)(2,1)}, u32[]{:S(2)}) copy-start(bf16[768,768]{1,0:T(8,128)(2,1)} %param.38) | copy-start | bytes 3538948
  (87 other events, 280.4 us)
Sparse Core Ops, SparseCore 0:
  21.5 62.7 all-gather.2
  185.2 117.5 reduce-scatter.1
  693.6 35.7 all-reduce.5

commit v2 on v0

--- a/solution.py
+++ b/solution.py
@@ -1,8 +1,11 @@
 import math
+import types
 
 import jax
 import jax.numpy as jnp
 from jax import lax
+from jax.experimental import pallas as pl
+from jax.experimental.pallas import tpu as pltpu
 from jax.sharding import PartitionSpec as P
 
 H = 12
@@ -134,7 +137,1219 @@
     return lax.dynamic_slice_in_dim(values, place * share, share, 1)
 
 
+MESH = pl.DeviceIdType.MESH
+D = 768
+PART = 48
+VMEM_BYTES = 66500 * 1000
+
+
+def places():
+    band, seq = lax.axis_index("band"), lax.axis_index("seq")
+    return lax.div(band, 2), lax.rem(band, 2), lax.div(seq, 2), lax.rem(seq, 2)
+
+
+def device(y, core, z, x):
+    return (y * 2 + core, z * 2 + x)
+
+
+def remote(src, dst, send, recv, target):
+    return pltpu.make_async_remote_copy(
+        src_ref=src, dst_ref=dst, send_sem=send, recv_sem=recv, device_id=target, device_id_type=MESH
+    )
+
+
+def greet(partners):
+    barrier = pltpu.get_barrier_semaphore()
+    for partner in partners:
+        pl.semaphore_signal(barrier, inc=1, device_id=partner, device_id_type=MESH)
+    pl.semaphore_wait(barrier, len(partners))
+
+
+class Spread:
+    def __init__(self, buffers, recv, up, down, across):
+        self.buffers, self.recv, self.up, self.down, self.across = buffers, recv, up, down, across
+        self.y, self.core, self.z, self.x = places()
+
+    def copies(self, slot, sems, at, target):
+        return [
+            remote(buf.at[slot], buf.at[slot], sems.at[i, at], self.recv.at[i, slot], target)
+            for i, buf in enumerate(self.buffers)
+        ]
+
+    def to_up(self, k):
+        return self.copies(
+            (self.z - k) * 2 + self.x, self.up, k, device(self.y, self.core, self.z + 1, self.x)
+        )
+
+    def to_down(self, k):
+        return self.copies(
+            (self.z + k) * 2 + self.x, self.down, k, device(self.y, self.core, self.z - 1, self.x)
+        )
+
+    def to_across(self, row):
+        return self.copies(
+            row * 2 + self.x, self.across, row, device(self.y, self.core, self.z, 1 - self.x)
+        )
+
+    def arrived(self, slot):
+        for copy in self.copies(slot, self.across, 0, device(self.y, self.core, self.z, 1 - self.x)):
+            copy.wait_recv()
+
+    def start(self):
+        z = self.z
+
+        @pl.when(z < 3)
+        def _():
+            for copy in self.to_up(0):
+                copy.start()
+
+        @pl.when(z > 0)
+        def _():
+            for copy in self.to_down(0):
+                copy.start()
+
+        for copy in self.to_across(z):
+            copy.start()
+
+    def relay(self, k):
+        z = self.z
+
+        @pl.when(z >= k)
+        def _():
+            self.arrived((z - k) * 2 + self.x)
+
+            @pl.when(z < 3)
+            def _():
+                for copy in self.to_up(k):
+                    copy.start()
+
+            for copy in self.to_across(z - k):
+                copy.start()
+
+        @pl.when(z + k <= 3)
+        def _():
+            self.arrived((z + k) * 2 + self.x)
+
+            @pl.when(z > 0)
+            def _():
+                for copy in self.to_down(k):
+                    copy.start()
+
+            for copy in self.to_across(z + k):
+                copy.start()
+
+    def finish(self):
+        z = self.z
+        for k in range(4):
+
+            @pl.when((z >= k) & (z < 3))
+            def _():
+                for copy in self.to_up(k):
+                    copy.wait_send()
+
+            @pl.when((z + k <= 3) & (z > 0))
+            def _():
+                for copy in self.to_down(k):
+                    copy.wait_send()
+
+            for copy in self.to_across(k):
+                copy.wait_send()
+
+
+def silu(values):
+    return values / (1.0 + jnp.exp(-values))
+
+
+def head_mask(half):
+    lane = lax.broadcasted_iota(jnp.int32, (1, 128), 1)
+    return (lane < 64) if half == 0 else (lane >= 64)
+
+
+def keep_head(tile, half):
+    return jnp.where(head_mask(half), tile, jnp.zeros_like(tile))
+
+
+def attend_kernel(
+    length_ref,
+    vector_ref,
+    frames_ref,
+    w_time_in_ref,
+    w_time_out_ref,
+    w_adaln_ref,
+    w_query_ref,
+    w_key_ref,
+    w_value_ref,
+    mod_ref,
+    time_ref,
+    qkv_ref,
+    attended_ref,
+    stats_ref,
+    gathered,
+    time_in,
+    time_out,
+    adaln,
+    projections,
+    load_sems,
+    recv,
+    up,
+    down,
+    across,
+):
+    y, core, z, x = places()
+    me = z * 2 + x
+    own = pltpu.make_async_copy(frames_ref, gathered.at[me], load_sems.at[0])
+    own.start()
+    loads = [
+        pltpu.make_async_copy(w_time_in_ref, time_in, load_sems.at[1]),
+        pltpu.make_async_copy(w_time_out_ref, time_out, load_sems.at[2]),
+    ]
+    loads += [
+        pltpu.make_async_copy(
+            w_adaln_ref.at[:, pl.ds(i * 1536, 1536)], adaln.at[i], load_sems.at[3 + i]
+        )
+        for i in range(3)
+    ]
+    loads += [
+        pltpu.make_async_copy(ref, projections.at[i], load_sems.at[6 + i])
+        for i, ref in enumerate((w_query_ref, w_key_ref, w_value_ref))
+    ]
+    for load in loads:
+        load.start()
+    neighbours = Spread([gathered], recv, up, down, across)
+    barrier = pltpu.get_barrier_semaphore()
+    pl.semaphore_signal(
+        barrier, inc=1, device_id=device(y, core, z, 1 - x), device_id_type=MESH
+    )
+
+    @pl.when(z < 3)
+    def _():
+        pl.semaphore_signal(barrier, inc=1, device_id=device(y, core, z + 1, x), device_id_type=MESH)
+
+    @pl.when(z > 0)
+    def _():
+        pl.semaphore_signal(barrier, inc=1, device_id=device(y, core, z - 1, x), device_id_type=MESH)
+
+    pl.semaphore_wait(barrier, 2 + lax.rem(lax.div(z + 1, 2), 2))
+    own.wait()
+    neighbours.start()
+    loads[0].wait()
+    first = product(vector_ref[...], time_in[...])
+    hidden = narrow(silu(first))
+    loads[1].wait()
+    second = product(hidden, time_out[...])
+    condition = narrow(silu(second))
+    time_ref[:, 0:D] = first[0:8]
+    time_ref[:, D : 2 * D] = second[0:8]
+    loads[2].wait()
+    mod_ref[:, 0:1536] = product(condition, adaln[0])[0:8]
+    neighbours.relay(1)
+    loads[3].wait()
+    mod_ref[:, 1536:3072] = product(condition, adaln[1])[0:8]
+    neighbours.relay(2)
+    loads[4].wait()
+    mod_ref[:, 3072:4608] = product(condition, adaln[2])[0:8]
+    neighbours.relay(3)
+    for load in loads[5:]:
+        load.wait()
+
+    def project(slot):
+        normed, unused = layer_norm(gathered[slot].astype(jnp.float32))
+        low = narrow(normed * (1.0 + mod_ref[0:1, D : 2 * D]) + mod_ref[0:1, 0:D])
+        for i in range(3):
+            qkv_ref[i, slot] = narrow(product(low, projections[i]))
+
+    def own_column(row, unused):
+        project(row * 2 + x)
+        return unused
+
+    def other_column(row, unused):
+        neighbours.arrived(row * 2 + 1 - x)
+        project(row * 2 + 1 - x)
+        return unused
+
+    lax.fori_loop(0, 4, own_column, 0)
+    lax.fori_loop(0, 4, other_column, 0)
+    length = length_ref[0]
+    key_valid = lax.broadcasted_iota(jnp.int32, (1, 1024), 1) < length
+    lane = lax.broadcasted_iota(jnp.int32, (1, 128), 1)
+
+    def pair(tile, stats):
+        at = pl.ds(pl.multiple_of(tile * 128, 128), 128)
+        query = qkv_ref[0, me, :, at]
+        keys = qkv_ref[1, :, :, at].reshape(1024, 128)
+        values = qkv_ref[2, :, :, at].reshape(1024, 128)
+        outs = []
+        for half in range(2):
+            scores = transposed_right(keep_head(query, half), keys) * 0.125
+            scores = jnp.where(key_valid, scores, masked_value)
+            row_max = jnp.max(scores, axis=1, keepdims=True)
+            expanded = jnp.exp(scores - row_max)
+            row_sum = jnp.sum(expanded, axis=1, keepdims=True)
+            outs.append(product(narrow(expanded), values) / row_sum)
+            stats = jnp.where(lane == tile * 2 + half, row_max + jnp.log(row_sum), stats)
+        attended_ref[:, at] = jnp.where(head_mask(0), outs[0], outs[1])
+        return stats
+
+    stats_ref[...] = lax.fori_loop(0, 6, pair, jnp.zeros((128, 128), jnp.float32))
+    neighbours.finish()
+
+
+def vmem(*shape, dtype=jnp.bfloat16):
+    return pltpu.VMEM(shape, dtype)
+
+
+def attend(length, vector, frames, weights):
+    dma = pltpu.SemaphoreType.DMA
+    in_vmem = pl.BlockSpec(memory_space=pltpu.VMEM)
+    in_place = pl.BlockSpec(memory_space=pl.ANY)
+    return pl.pallas_call(
+        attend_kernel,
+        out_shape=(
+            jax.ShapeDtypeStruct((8, 6 * D), jnp.float32),
+            jax.ShapeDtypeStruct((8, 2 * D), jnp.float32),
+            jax.ShapeDtypeStruct((3, 8, 128, D), jnp.bfloat16),
+            jax.ShapeDtypeStruct((128, D), jnp.float32),
+            jax.ShapeDtypeStruct((128, 128), jnp.float32),
+        ),
+        in_specs=[pl.BlockSpec(memory_space=pltpu.SMEM), in_vmem] + [in_place] * 7,
+        out_specs=(in_vmem,) * 5,
+        scratch_shapes=[
+            vmem(8, 128, D),
+            vmem(256, D),
+            vmem(D, D),
+            vmem(3, D, 1536),
+            vmem(3, D, D),
+            dma((9,)),
+            dma((1, 8)),
+            dma((1, 4)),
+            dma((1, 4)),
+            dma((1, 4)),
+        ],
+        compiler_params=pltpu.CompilerParams(
+            collective_id=1, has_side_effects=True, vmem_limit_bytes=VMEM_BYTES
+        ),
+    )(length, vector, frames, *weights)
+
+
+PRODUCTS = (
+    [(1 + j, 4) for j in range(4)]
+    + [(0, j) for j in range(4)]
+    + [(5, 5), (6, 6), (9, 8), (9, 9), (7, 7)]
+    + [(8, 10), (8, 11), (8, 12)]
+)
+LEFTS = 9
+RIGHTS = 13
+TEXT_UNIT = 9
+SLOTS = 4
+LATER = (0, 1, 3, 5, 7, 8)
+IN_VMEM = [
+    "mask",
+    "frames",
+    "cotangent",
+    "text",
+    "gain",
+    "mod",
+    "time",
+    "vector",
+    "qkv",
+    "attended",
+    "stats",
+]
+IN_PLACE = [
+    "hbm_out",
+    "hbm_cross_query",
+    "hbm_cross_key",
+    "hbm_cross_value",
+    "hbm_cross_out",
+    "hbm_mlp_in",
+    "hbm_mlp_out",
+    "hbm_query",
+    "hbm_key",
+    "hbm_value",
+    "hbm_adaln",
+    "hbm_time_out",
+]
+OUT_VMEM = [
+    "block_out",
+    "grad_frames",
+    "grad_text",
+    "gain_sum",
+    "conditions",
+    "hiddens",
+    "vectors",
+    "grad_mods",
+    "grad_time_outs",
+    "grad_time_firsts",
+]
+OUT_PLACE = ["pieces"]
+
+
+def block_scratch():
+    n = len(PRODUCTS)
+    sem = lambda *shape: pltpu.SemaphoreType.DMA(shape)
+    f32 = jnp.float32
+    return dict(
+        square=vmem(9, D, D),
+        mlp_in=vmem(D, 4 * D),
+        mlp_out=vmem(4 * D, D),
+        adaln_high=vmem(D, 2 * D),
+        load_sems=sem(16),
+        lefts=vmem(LEFTS, 128, D),
+        gt=vmem(RIGHTS, 2, 2, 192, 128),
+        grecv=vmem(RIGHTS, 2, 192, 128),
+        lrecv=vmem(LEFTS, 128, D),
+        pbuf=vmem(SLOTS, 2, 192, D),
+        precv=vmem(n, 192, D),
+        qbuf=vmem(SLOTS, 2, 192, 384),
+        qrecv=vmem(n, 192, 384),
+        rbuf=vmem(SLOTS, 4, PART, 384),
+        rrecv=vmem(n, 4, PART, 384),
+        final=vmem(n, 2, 2, PART, 384),
+        ls=sem(LEFTS),
+        lr=sem(LEFTS),
+        gs=sem(RIGHTS),
+        gr=sem(RIGHTS),
+        ps=sem(n),
+        pr=sem(n),
+        qs=sem(n),
+        qr=sem(n),
+        rs=sem(n, 4),
+        rr=sem(n, 4),
+        fs=sem(n, 2),
+        fr=sem(n, 2),
+        out_sems=sem(n),
+        heads=vmem(8, 128, D),
+        rowstats=vmem(8, 32, 128, dtype=f32),
+        sp_recv=sem(2, 8),
+        sp_up=sem(2, 4),
+        sp_down=sem(2, 4),
+        sp_across=sem(2, 4),
+        times=vmem(4, 8, 2 * D, dtype=f32),
+        vecs=vmem(4, 16, 256),
+        ts=sem(2, 4),
+        tr=sem(2, 4),
+        text_part=vmem(8, 16, D, dtype=f32),
+        text_send=vmem(8, 16, D),
+        text_recv=vmem(8, 16, D),
+        xs=sem(8),
+        xr=sem(8),
+        sums=vmem(8, D, dtype=f32),
+        sums_recv=vmem(8, 8, D, dtype=f32),
+        ss=sem(8),
+        sr=sem(8),
+        clip_sums=vmem(4, 8, D, dtype=f32),
+        cs=sem(4),
+        cr=sem(4),
+        proj=vmem(128, D, dtype=f32),
+        middle=vmem(128, D, dtype=f32),
+        normed_cross=vmem(128, D, dtype=f32),
+        normed_mlp=vmem(128, D, dtype=f32),
+        after=vmem(128, D, dtype=f32),
+        pre=vmem(4, 128, D, dtype=f32),
+        acc=vmem(128, D, dtype=f32),
+        grad_pre=vmem(4, 128, D),
+        grad_mlp=vmem(128, D),
+        cross_q=vmem(128, D),
+        cross_k=vmem(128, D),
+        cross_v=vmem(128, D),
+        cross_probs=vmem(12, 128, 128, dtype=f32),
+        grad_heads=vmem(128, D),
+        grad_q=vmem(128, D),
+        grad_k=vmem(128, D),
+        grad_v=vmem(128, D),
+    )
+
+
+def gelu(v):
+    inner = jnp.tanh(0.7978845608028654 * (v + 0.044715 * v * v * v))
+    return 0.5 * v * (1.0 + inner)
+
+
+def gelu_slope(v):
+    inner = jnp.tanh(0.7978845608028654 * (v + 0.044715 * v * v * v))
+    return 0.5 * (1.0 + inner) + 0.5 * v * (1.0 - inner * inner) * 0.7978845608028654 * (
+        1.0 + 3 * 0.044715 * v * v
+    )
+
+
+def silu_slope(v):
+    gate = 1.0 / (1.0 + jnp.exp(-v))
+    return gate * (1.0 + v * (1.0 - gate))
+
+
+class Sums:
+    def __init__(self, r):
+        self.r = r
+        self.y, self.core, self.z, self.x = y, core, z, x = places()
+        self.across = device(y, core, z, 1 - x)
+        self.clips = [
+            None,
+            device(y, 1 - core, z, x),
+            device(1 - y, core, z, x),
+            device(1 - y, 1 - core, z, x),
+        ]
+        self.done = 0
+
+    def left_copy(self, u):
+        r = self.r
+        return remote(r.lefts.at[u], r.lrecv.at[u], r.ls.at[u], r.lr.at[u], self.across)
+
+    def right_copy(self, u):
+        r = self.r
+        return remote(r.gt.at[u, 1 - self.x], r.grecv.at[u], r.gs.at[u], r.gr.at[u], self.across)
+
+    def core_copy(self, i):
+        r = self.r
+        mine = r.pbuf.at[i % SLOTS, 1 - self.core]
+        return remote(mine, r.precv.at[i], r.ps.at[i], r.pr.at[i], self.clips[1])
+
+    def y_copy(self, i):
+        r = self.r
+        mine = r.qbuf.at[i % SLOTS, 1 - self.y]
+        return remote(mine, r.qrecv.at[i], r.qs.at[i], r.qr.at[i], self.clips[2])
+
+    def z_copy(self, i, k):
+        r = self.r
+        to = lax.rem(self.z + k, 4)
+        return remote(
+            r.rbuf.at[i % SLOTS, to],
+            r.rrecv.at[i, k],
+            r.rs.at[i, k],
+            r.rr.at[i, k],
+            device(self.y, self.core, to, self.x),
+        )
+
+    def last_y_copy(self, i):
+        r = self.r
+        piece = r.final.at[i, self.core, self.y]
+        return remote(piece, piece, r.fs.at[i, 0], r.fr.at[i, 0], self.clips[2])
+
+    def last_core_copy(self, i):
+        r = self.r
+        piece = r.final.at[i, self.core]
+        return remote(piece, piece, r.fs.at[i, 1], r.fr.at[i, 1], self.clips[1])
+
+    def out_copy(self, i):
+        r = self.r
+        return pltpu.make_async_copy(r.final.at[i], r.pieces.at[i], r.out_sems.at[i])
+
+    def post_left(self, u, values):
+        self.r.lefts[u] = values
+        self.left_copy(u).start()
+
+    def post_right(self, u, values):
+        turned = narrow(jnp.transpose(values.astype(jnp.float32)))
+        for s in range(8):
+            for c in range(2):
+                at = s * 96 + c * PART
+                self.r.gt[u, s % 2, c, pl.ds((s // 2) * PART, PART), :] = turned[at : at + PART]
+        self.right_copy(u).start()
+
+    def multiply(self, i):
+        r, x = self.r, self.x
+        left, right = PRODUCTS[i]
+        if left != TEXT_UNIT and (i == 0 or PRODUCTS[i - 1][0] != left):
+            self.left_copy(left).wait_recv()
+        if i == 0 or PRODUCTS[i - 1][1] != right:
+            self.right_copy(right).wait_recv()
+        if i >= SLOTS:
+            self.core_copy(i - SLOTS).wait_send()
+        for c in range(2):
+            mine, theirs = r.gt[right, x, c], r.grecv[right, c]
+            if left == TEXT_UNIT:
+                both = narrow(mine.astype(jnp.float32) + theirs.astype(jnp.float32))
+                part = product(both, r.text[...])
+            else:
+                part = product(
+                    jnp.concatenate([mine, theirs], axis=1),
+                    jnp.concatenate([r.lefts[left], r.lrecv[left]], axis=0),
+                )
+            r.pbuf[i % SLOTS, c] = narrow(part)
+        self.core_copy(i).start()
+
+    def add_core(self, i):
+        r = self.r
+        self.core_copy(i).wait_recv()
+        if i >= SLOTS:
+            self.y_copy(i - SLOTS).wait_send()
+        total = narrow(
+            r.pbuf[i % SLOTS, self.core].astype(jnp.float32) + r.precv[i].astype(jnp.float32)
+        )
+        r.qbuf[i % SLOTS, 0] = total[:, :384]
+        r.qbuf[i % SLOTS, 1] = total[:, 384:]
+        self.y_copy(i).start()
+
+    def add_y(self, i):
+        r = self.r
+        self.y_copy(i).wait_recv()
+        if i >= SLOTS:
+            for k in (1, 2, 3):
+                self.z_copy(i - SLOTS, k).wait_send()
+        total = narrow(
+            r.qbuf[i % SLOTS, self.y].astype(jnp.float32) + r.qrecv[i].astype(jnp.float32)
+        )
+        for k in range(4):
+            r.rbuf[i % SLOTS, k] = total[k * PART : (k + 1) * PART]
+        for k in (1, 2, 3):
+            self.z_copy(i, k).start()
+
+    def add_z(self, i):
+        r = self.r
+        for k in (1, 2, 3):
+            self.z_copy(i, k).wait_recv()
+        total = r.rbuf[i % SLOTS, self.z].astype(jnp.float32)
+        for k in (1, 2, 3):
+            total = total + r.rrecv[i, k].astype(jnp.float32)
+        r.final[i, self.core, self.y] = narrow(total)
+        self.last_y_copy(i).start()
+
+    def pass_on(self, i):
+        self.last_y_copy(i).wait_recv()
+        self.last_core_copy(i).start()
+
+    def output(self, i):
+        self.last_core_copy(i).wait_recv()
+        self.out_copy(i).start()
+
+    def step(self, times=1):
+        n = len(PRODUCTS)
+        stages = (
+            self.multiply,
+            self.add_core,
+            self.add_y,
+            self.add_z,
+            self.pass_on,
+            self.output,
+        )
+        for unused in range(times):
+            for later, stage in reversed(list(zip(LATER, stages))):
+                if 0 <= self.done - later < n:
+                    stage(self.done - later)
+            self.done += 1
+
+    def finish(self):
+        n = len(PRODUCTS)
+        while self.done < n + LATER[-1]:
+            self.step()
+        for u in range(LEFTS):
+            self.left_copy(u).wait_send()
+        for u in range(RIGHTS):
+            self.right_copy(u).wait_send()
+        for i in range(n):
+            if i >= n - SLOTS:
+                self.core_copy(i).wait_send()
+                self.y_copy(i).wait_send()
+                for k in (1, 2, 3):
+                    self.z_copy(i, k).wait_send()
+            self.last_y_copy(i).wait_send()
+            self.last_core_copy(i).wait_send()
+            self.out_copy(i).wait()
+
+
+def block_kernel(length_ref, *refs):
+    names = IN_VMEM + IN_PLACE + OUT_VMEM + OUT_PLACE + list(block_scratch())
+    r = types.SimpleNamespace(**dict(zip(names, refs, strict=True)))
+    y, core, z, x = places()
+    me, band = z * 2 + x, y * 2 + core
+    peers = [device(y, core, lax.div(s, 2), lax.rem(s, 2)) for s in [lax.rem(me + k, 8) for k in range(8)]]
+    sums = Sums(r)
+
+    def load(i, src, dst):
+        return pltpu.make_async_copy(src, dst, r.load_sems.at[i])
+
+    squares = (
+        r.hbm_out,
+        r.hbm_cross_query,
+        r.hbm_cross_key,
+        r.hbm_cross_value,
+        r.hbm_cross_out,
+        r.hbm_query,
+        r.hbm_key,
+        r.hbm_value,
+        r.hbm_time_out,
+    )
+    OUT, CQ, CK, CV, CO, WQ, WK, WV, TIME = range(9)
+    loads = [load(i, ref, r.square.at[i]) for i, ref in enumerate(squares)]
+    loads.append(load(9, r.hbm_mlp_in, r.mlp_in))
+    loads.append(load(10, r.hbm_mlp_out, r.mlp_out))
+    loads.append(load(11, r.hbm_adaln.at[:, pl.ds(3072, 1536)], r.adaln_high))
+    adaln_low = load(12, r.hbm_adaln.at[:, pl.ds(0, 3072)], r.mlp_in)
+    for i in (0, 2, 3, 1, 4, 9, 10, 5, 6, 7, 8, 11):
+        loads[i].start()
+    greet(peers[1:] + sums.clips[1:])
+
+    def clip_copy(refs, sems, recvs, j):
+        return [
+            remote(ref.at[band], ref.at[band], sems.at[i, j], recvs.at[i, j], sums.clips[j])
+            for i, ref in enumerate(refs)
+        ]
+
+    r.times[band] = r.time[...]
+    r.vecs[band] = r.vector[...]
+    for j in (1, 2, 3):
+        for copy in clip_copy((r.times, r.vecs), r.ts, r.tr, j):
+            copy.start()
+
+    length = length_ref[0]
+
+    def row_valid():
+        return lax.broadcasted_iota(jnp.int32, (128, 1), 0) + me * 128 < length
+
+    def modulation(i):
+        return r.mod[0:1, i * D : (i + 1) * D]
+
+    def over_rows(values):
+        return jnp.sum(values, axis=0, keepdims=True)
+
+    lane = lax.broadcasted_iota(jnp.int32, (1, 128), 1)
+    text_valid = r.mask[...] != 0
+    gain = r.gain[...].astype(jnp.float32)
+
+    def tile_at(tile):
+        return pl.ds(pl.multiple_of(tile * 128, 128), 128)
+
+    normed, unused = layer_norm(r.frames[...].astype(jnp.float32))
+    sums.post_left(8, narrow(normed * (1.0 + modulation(1)) + modulation(0)))
+    sums.post_left(7, narrow(r.attended[...]))
+    r.grad_mlp[...] = narrow(
+        modulation(5) * jnp.where(row_valid(), r.cotangent[...].astype(jnp.float32), 0.0)
+    )
+    sums.post_right(4, r.grad_mlp[...])
+    loads[OUT].wait()
+    r.proj[...] = product(r.lefts[7], r.square[OUT])
+    r.middle[...] = r.frames[...].astype(jnp.float32) + modulation(2) * r.proj[...]
+    normed, scaling_cross = layer_norm(r.middle[...])
+    r.normed_cross[...] = normed
+    sums.post_left(6, narrow(normed * gain))
+    loads[CK].wait()
+    r.cross_k[...] = narrow(product(r.text[...], r.square[CK]))
+    loads[CV].wait()
+    r.cross_v[...] = narrow(product(r.text[...], r.square[CV]))
+    loads[CQ].wait()
+    r.cross_q[...] = narrow(product(r.lefts[6], r.square[CQ]))
+
+    def cross_pair(tile, unused):
+        at = tile_at(tile)
+        query, keys, values = r.cross_q[:, at], r.cross_k[:, at], r.cross_v[:, at]
+        outs = []
+        for half in range(2):
+            scores = transposed_right(keep_head(query, half), keys) * 0.125
+            scores = jnp.where(text_valid, scores, masked_value)
+            row_max = jnp.max(scores, axis=1, keepdims=True)
+            total = row_max + jnp.log(jnp.sum(jnp.exp(scores - row_max), axis=1, keepdims=True))
+            probs = jnp.exp(scores - total)
+            r.cross_probs[tile * 2 + half] = probs
+            outs.append(product(narrow(probs), values))
+        r.lefts[5, :, at] = narrow(jnp.where(head_mask(0), outs[0], outs[1]))
+        return unused
+
+    lax.fori_loop(0, 6, cross_pair, 0)
+    sums.left_copy(5).start()
+    loads[CO].wait()
+    r.after[...] = r.middle[...] + product(r.lefts[5], r.square[CO])
+    normed, scaling_mlp = layer_norm(r.after[...])
+    r.normed_mlp[...] = normed
+    sums.post_left(0, narrow(normed * (1.0 + modulation(4)) + modulation(3)))
+    loads[9].wait()
+    loads[10].wait()
+    for j in range(4):
+        pre = product(r.lefts[0], r.mlp_in[:, j * D : (j + 1) * D])
+        r.pre[j] = pre
+        sums.post_left(1 + j, narrow(gelu(pre)))
+        part = product(r.lefts[1 + j], r.mlp_out[j * D : (j + 1) * D, :])
+        r.acc[...] = part if j == 0 else r.acc[...] + part
+    frames = r.frames[...].astype(jnp.float32)
+    r.block_out[...] = narrow(
+        jnp.where(row_valid(), r.after[...] + modulation(5) * r.acc[...], frames)
+    )
+    grad_res = jnp.where(row_valid(), r.cotangent[...].astype(jnp.float32), 0.0)
+    r.sums[5:6, :] = over_rows(grad_res * r.acc[...])
+    for j in range(4):
+        slope = gelu_slope(r.pre[j])
+        grad = narrow(slope * transposed_right(r.grad_mlp[...], r.mlp_out[j * D : (j + 1) * D, :]))
+        r.grad_pre[j] = grad
+        for part in range(2):
+            s = j * 2 + part
+            turned = narrow(
+                jnp.transpose(grad[:, part * 384 : (part + 1) * 384].astype(jnp.float32))
+            )
+            for u in range(4):
+                for c in range(2):
+                    at = u * 96 + c * PART
+                    r.gt[u, s % 2, c, pl.ds((s // 2) * PART, PART), :] = turned[at : at + PART]
+    for u in range(4):
+        sums.right_copy(u).start()
+    for j in range(4):
+        part = transposed_right(r.grad_pre[j], r.mlp_in[:, j * D : (j + 1) * D])
+        r.acc[...] = part if j == 0 else r.acc[...] + part
+    adaln_low.start()
+    r.sums[3:4, :] = over_rows(r.acc[...])
+    r.sums[4:5, :] = over_rows(r.acc[...] * r.normed_mlp[...])
+    grad_res = jnp.where(row_valid(), r.cotangent[...].astype(jnp.float32), 0.0)
+    r.after[...] = grad_res + norm_back(
+        r.normed_mlp[...], scaling_mlp, r.acc[...] * (1.0 + modulation(4))
+    )
+    low = narrow(r.after[...])
+    sums.post_right(5, low)
+    r.grad_heads[...] = narrow(transposed_right(low, r.square[CO]))
+
+    def cross_pair_back(tile, unused):
+        at = tile_at(tile)
+        query, keys, values = r.cross_q[:, at], r.cross_k[:, at], r.cross_v[:, at]
+        grad = r.grad_heads[:, at]
+        outs = []
+        for half in range(2):
+            probs = r.cross_probs[tile * 2 + half]
+            grad_probs = transposed_right(keep_head(grad, half), values)
+            inner = jnp.sum(probs * grad_probs, axis=1, keepdims=True)
+            scores = narrow(probs * (grad_probs - inner)).astype(jnp.float32)
+            outs.append(
+                (
+                    product(narrow(scores), keys),
+                    product(narrow(jnp.transpose(scores)), query),
+                    product(narrow(jnp.transpose(probs)), grad),
+                )
+            )
+        grad_q, grad_k, grad_v = [jnp.where(head_mask(0), a, b) for a, b in zip(*outs)]
+        r.grad_q[:, at] = narrow(grad_q * 0.125)
+        r.grad_k[:, at] = narrow(grad_k * 0.125)
+        r.grad_v[:, at] = narrow(grad_v)
+        return unused
+
+    lax.fori_loop(0, 6, cross_pair_back, 0)
+    sums.post_right(6, r.grad_q[...])
+    grad_cross_in = transposed_right(r.grad_q[...], r.square[CQ])
+    r.sums[6:7, :] = over_rows(grad_cross_in * r.normed_cross[...])
+    r.sums[7:8, :] = jnp.zeros((1, D), jnp.float32)
+    r.middle[...] = r.after[...] + norm_back(
+        r.normed_cross[...], scaling_cross, grad_cross_in * gain
+    )
+    low = narrow(modulation(2) * r.middle[...])
+    grad_heads = narrow(transposed_right(low, r.square[OUT]))
+    r.heads[me] = grad_heads
+    products = grad_heads.astype(jnp.float32) * r.attended[...]
+    delta = jnp.zeros((128, 128), jnp.float32)
+    for h in range(12):
+        tile = products[:, (h // 2) * 128 : (h // 2 + 1) * 128]
+        inner = jnp.sum(jnp.where(head_mask(h % 2), tile, 0.0), axis=1, keepdims=True)
+        delta = jnp.where(lane == h, inner, delta)
+    r.rowstats[me] = jnp.concatenate(
+        [jnp.transpose(r.stats[...])[:16], jnp.transpose(delta)[:16]], axis=0
+    )
+    spread = Spread([r.heads, r.rowstats], r.sp_recv, r.sp_up, r.sp_down, r.sp_across)
+    spread.start()
+    sums.post_right(7, low)
+    r.sums[2:3, :] = over_rows(r.middle[...] * r.proj[...])
+    sums.post_right(8, r.grad_k[...])
+    sums.post_right(9, r.grad_v[...])
+    text_grad = transposed_right(r.grad_k[...], r.square[CK]) + transposed_right(
+        r.grad_v[...], r.square[CV]
+    )
+    for s in range(8):
+        r.text_part[s] = text_grad[s * 16 : (s + 1) * 16]
+        r.text_send[s] = narrow(text_grad[s * 16 : (s + 1) * 16])
+
+    def text_copy(k):
+        return remote(
+            r.text_send.at[lax.rem(me + k, 8)], r.text_recv.at[k], r.xs.at[k], r.xr.at[k], peers[k]
+        )
+
+    for k in range(1, 8):
+        text_copy(k).start()
+    spread.relay(1)
+    key_valid = lax.broadcasted_iota(jnp.int32, (1, 1024), 1) < length
+
+    def query_pair(tile, unused):
+        at = tile_at(tile)
+        query, grad = r.qkv[0, me, :, at], r.heads[me, :, at]
+        keys = r.qkv[1, :, :, at].reshape(1024, 128)
+        values = r.qkv[2, :, :, at].reshape(1024, 128)
+        tile_product = grad.astype(jnp.float32) * r.attended[:, at]
+        outs = []
+        for half in range(2):
+            scores = transposed_right(keep_head(query, half), keys) * 0.125
+            scores = jnp.where(key_valid, scores, masked_value)
+            total = jnp.sum(
+                jnp.where(lane == tile * 2 + half, r.stats[...], 0.0), axis=1, keepdims=True
+            )
+            inner = jnp.sum(jnp.where(head_mask(half), tile_product, 0.0), axis=1, keepdims=True)
+            grad_probs = transposed_right(keep_head(grad, half), values)
+            outs.append(product(narrow(jnp.exp(scores - total) * (grad_probs - inner)), keys))
+        r.grad_q[:, at] = narrow(jnp.where(head_mask(0), outs[0], outs[1]) * 0.125)
+        return unused
+
+    lax.fori_loop(0, 2, query_pair, 0)
+    spread.relay(2)
+    lax.fori_loop(2, 4, query_pair, 0)
+    spread.relay(3)
+    lax.fori_loop(4, 6, query_pair, 0)
+    sums.post_right(10, r.grad_q[...])
+    sums.step(6)
+    for row in range(4):
+        spread.arrived(row * 2 + 1 - x)
+
+    def key_pair(tile, unused):
+        at = tile_at(tile)
+        key, value = r.qkv[1, me, :, at], r.qkv[2, me, :, at]
+        queries = r.qkv[0, :, :, at].reshape(1024, 128)
+        grads = r.heads[:, :, at].reshape(1024, 128)
+        outs = []
+        for half in range(2):
+            h = tile * 2 + half
+            total = jnp.concatenate([r.rowstats[s, pl.ds(h, 1), :] for s in range(8)], axis=1)
+            inner = jnp.concatenate([r.rowstats[s, pl.ds(16 + h, 1), :] for s in range(8)], axis=1)
+            scores = transposed_right(keep_head(key, half), queries) * 0.125
+            scores = jnp.where(row_valid(), scores, masked_value)
+            probs = jnp.exp(scores - total)
+            grad_probs = transposed_right(keep_head(value, half), grads)
+            grad_scores = narrow(probs * (grad_probs - inner))
+            outs.append((product(grad_scores, queries), product(narrow(probs), grads)))
+        grad_k, grad_v = [jnp.where(head_mask(0), a, b) for a, b in zip(*outs)]
+        r.grad_k[:, at] = narrow(grad_k * 0.125)
+        r.grad_v[:, at] = narrow(grad_v)
+        return unused
+
+    lax.fori_loop(0, 6, key_pair, 0)
+    sums.post_right(11, r.grad_k[...])
+    sums.post_right(12, r.grad_v[...])
+    for i in (WQ, WK, WV):
+        loads[i].wait()
+    grad_in = (
+        transposed_right(r.grad_q[...], r.square[WQ])
+        + transposed_right(r.grad_k[...], r.square[WK])
+        + transposed_right(r.grad_v[...], r.square[WV])
+    )
+    r.acc[...] = grad_in
+    normed, scaling = layer_norm(r.frames[...].astype(jnp.float32))
+    r.sums[0:1, :] = over_rows(r.acc[...])
+    r.sums[1:2, :] = over_rows(r.acc[...] * normed)
+
+    def sums_copy(k):
+        return remote(r.sums, r.sums_recv.at[k], r.ss.at[k], r.sr.at[k], peers[k])
+
+    for k in range(1, 8):
+        sums_copy(k).start()
+    grads = r.middle[...] + norm_back(normed, scaling, r.acc[...] * (1.0 + modulation(1)))
+    r.grad_frames[...] = narrow(
+        jnp.where(row_valid(), grads, r.cotangent[...].astype(jnp.float32))
+    )
+    sums.step(4)
+    total = r.sums[...]
+    for k in range(1, 8):
+        sums_copy(k).wait_recv()
+        total = total + r.sums_recv[k]
+    r.clip_sums[band] = total
+
+    def total_copy(j):
+        return remote(
+            r.clip_sums.at[band], r.clip_sums.at[band], r.cs.at[j], r.cr.at[j], sums.clips[j]
+        )
+
+    for j in (1, 2, 3):
+        total_copy(j).start()
+    sums.step(3)
+    for j in (1, 2, 3):
+        total_copy(j).wait_recv()
+        for copy in clip_copy((r.times, r.vecs), r.ts, r.tr, j):
+            copy.wait_recv()
+    r.gain_sum[0:1, :] = (r.clip_sums[0, 6:7] + r.clip_sums[1, 6:7]) + (
+        r.clip_sums[2, 6:7] + r.clip_sums[3, 6:7]
+    )
+    r.gain_sum[1:8, :] = jnp.zeros((7, D), jnp.float32)
+
+    def by_clip(pieces):
+        return jnp.concatenate(pieces + [jnp.zeros((12, pieces[0].shape[1]), jnp.float32)], axis=0)
+
+    for i in range(6):
+        r.grad_mods[:, i * D : (i + 1) * D] = narrow(
+            by_clip([r.clip_sums[b, i : i + 1] for b in range(4)])
+        )
+    firsts = by_clip([r.times[b, 0:1, 0:D] for b in range(4)])
+    seconds = by_clip([r.times[b, 0:1, D : 2 * D] for b in range(4)])
+    r.hiddens[...] = narrow(silu(firsts))
+    r.conditions[...] = narrow(silu(seconds))
+    for b in range(4):
+        r.vectors[b] = r.vecs[b]
+    adaln_low.wait()
+    loads[11].wait()
+    loads[TIME].wait()
+    grad_condition = transposed_right(r.grad_mods[:, :3072], r.mlp_in[...]) + transposed_right(
+        r.grad_mods[:, 3072:], r.adaln_high[...]
+    )
+    low = narrow(silu_slope(seconds) * grad_condition)
+    r.grad_time_outs[...] = low
+    r.grad_time_firsts[...] = silu_slope(firsts) * transposed_right(low, r.square[TIME])
+    total = r.text_part[me]
+    for k in range(1, 8):
+        text_copy(k).wait_recv()
+        total = total + r.text_recv[k].astype(jnp.float32)
+    r.grad_text[...] = total
+    sums.finish()
+    spread.finish()
+    for k in range(1, 8):
+        text_copy(k).wait_send()
+        sums_copy(k).wait_send()
+    for j in (1, 2, 3):
+        total_copy(j).wait_send()
+        for copy in clip_copy((r.times, r.vecs), r.ts, r.tr, j):
+            copy.wait_send()
+
+
+def block(length, vmem_args, place_args):
+    in_vmem = pl.BlockSpec(memory_space=pltpu.VMEM)
+    in_place = pl.BlockSpec(memory_space=pl.ANY)
+    shape = jax.ShapeDtypeStruct
+    f32, bf16 = jnp.float32, jnp.bfloat16
+    return pl.pallas_call(
+        block_kernel,
+        out_shape=(
+            shape((128, D), bf16),
+            shape((128, D), bf16),
+            shape((16, D), f32),
+            shape((8, D), f32),
+            shape((16, D), bf16),
+            shape((16, D), bf16),
+            shape((4, 16, 256), bf16),
+            shape((16, 6 * D), bf16),
+            shape((16, D), bf16),
+            shape((16, D), f32),
+            shape((len(PRODUCTS), 2, 2, PART, 384), bf16),
+        ),
+        in_specs=[pl.BlockSpec(memory_space=pltpu.SMEM)]
+        + [in_vmem] * len(IN_VMEM)
+        + [in_place] * len(IN_PLACE),
+        out_specs=(in_vmem,) * len(OUT_VMEM) + (in_place,) * len(OUT_PLACE),
+        scratch_shapes=list(block_scratch().values()),
+        compiler_params=pltpu.CompilerParams(
+            collective_id=0, has_side_effects=True, vmem_limit_bytes=VMEM_BYTES
+        ),
+    )(length, *vmem_args, *place_args)
+
+
+SQUARES = (8, 9, 12, 10, 11, 13, 14, 15)
+FINAL_IN = [
+    "pieces",
+    "block_out",
+    "grad_frames",
+    "grad_text",
+    "gain_sum",
+    "conditions",
+    "hiddens",
+    "vectors",
+    "grad_mods",
+    "grad_time_outs",
+    "grad_time_firsts",
+]
+FINAL_SHAPES = (
+    [((128, D), jnp.bfloat16), ((128, D), jnp.bfloat16), ((16, D), jnp.float32)]
+    + [((96, 256), jnp.float32), ((96, D), jnp.float32), ((576, D), jnp.float32)]
+    + [((1, 96), jnp.float32), ((D, 384), jnp.float32), ((96, 4 * D), jnp.float32)]
+    + [((96, D), jnp.float32)] * 8
+)
+
+
+def final_kernel(*refs):
+    r = types.SimpleNamespace(**dict(zip(FINAL_IN, refs)))
+    count = len(FINAL_SHAPES)
+    rest = refs[len(FINAL_IN) :]
+    outs, staged, (turned_mods, turned_small, sems) = rest[:count], rest[count : 2 * count], rest[2 * count :]
+    seq = lax.axis_index("seq")
+
+    def put(i, values):
+        staged[i][...] = values
+        copy(i).start()
+
+    def copy(i):
+        return pltpu.make_async_copy(staged[i], outs[i], sems.at[i])
+
+    def whole(p):
+        return jnp.concatenate(
+            [jnp.concatenate([r.pieces[p, c, h] for h in range(2)], axis=1) for c in range(2)],
+            axis=0,
+        ).astype(jnp.float32)
+
+    put(7, jnp.transpose(jnp.concatenate([whole(4 + j) for j in range(4)], axis=0)))
+    for j in range(4):
+        staged[8][:, j * D : (j + 1) * D] = whole(j)
+    copy(8).start()
+    for j, p in enumerate(SQUARES):
+        put(9 + j, whole(p))
+    put(0, r.block_out[...])
+    put(1, r.grad_frames[...])
+    put(2, r.grad_text[...])
+    turned_mods[...] = jnp.transpose(r.grad_mods[...].astype(jnp.float32))
+    put(
+        5,
+        product(
+            narrow(turned_mods[pl.ds(pl.multiple_of(seq * 576, 64), 576), :]), r.conditions[...]
+        ),
+    )
+    own = pl.ds(pl.multiple_of(seq * 96, 32), 96)
+    turned_small[0] = jnp.transpose(r.grad_time_outs[...].astype(jnp.float32))
+    put(4, product(narrow(turned_small[0, own, :]), r.hiddens[...]))
+    turned_small[1] = jnp.transpose(r.grad_time_firsts[...])
+    rows = [r.vectors[b, 0:1].astype(jnp.float32) for b in range(4)]
+    vectors = jnp.concatenate(rows + [jnp.zeros((12, 256), jnp.float32)], axis=0)
+    put(
+        3,
+        jnp.dot(
+            turned_small[1, own, :],
+            vectors,
+            precision=lax.Precision.HIGHEST,
+            preferred_element_type=jnp.float32,
+        ),
+    )
+    gains = jnp.concatenate([r.gain_sum[...], jnp.zeros((8, D), jnp.float32)], axis=0)
+    turned_small[2] = jnp.transpose(gains)
+    put(6, jnp.transpose(turned_small[2, own, :])[0:1])
+    for i in range(count):
+        copy(i).wait()
+
+
+def finish(values):
+    in_vmem = pl.BlockSpec(memory_space=pltpu.VMEM)
+    in_place = pl.BlockSpec(memory_space=pl.ANY)
+    return pl.pallas_call(
+        final_kernel,
+        out_shape=tuple(jax.ShapeDtypeStruct(*shape) for shape in FINAL_SHAPES),
+        in_specs=[in_vmem] * len(FINAL_IN),
+        out_specs=(in_place,) * len(FINAL_SHAPES),
+        scratch_shapes=[pltpu.VMEM(*shape) for shape in FINAL_SHAPES]
+        + [
+            vmem(6 * D, 16, dtype=jnp.float32),
+            vmem(3, D, 16, dtype=jnp.float32),
+            pltpu.SemaphoreType.DMA((len(FINAL_SHAPES),)),
+        ],
+        compiler_params=pltpu.CompilerParams(vmem_limit_bytes=VMEM_BYTES),
+    )(*values)
+
+
 def on_device(
+    frames,
+    text,
+    timesteps,
+    frame_lengths,
+    text_mask,
+    cotangent,
+    w_time_in,
+    w_time_out,
+    w_adaln,
+    w_query,
+    w_key,
+    w_value,
+    w_attn_out,
+    cross_gain,
+    w_cross_query,
+    w_cross_key,
+    w_cross_value,
+    w_cross_out,
+    w_mlp_in,
+    w_mlp_out,
+):
+    vector = jnp.broadcast_to(narrow(time_embed(timesteps, w_time_in.shape[0])), (16, 256))
+    mod, time, qkv, attended, stats = attend(
+        frame_lengths,
+        vector,
+        frames[0],
+        (w_time_in, w_time_out, w_adaln, w_query, w_key, w_value),
+    )
+    (
+        block_out,
+        grad_frames,
+        grad_text,
+        gain_sum,
+        conditions,
+        hiddens,
+        vectors,
+        grad_mods,
+        grad_time_outs,
+        grad_time_firsts,
+        pieces,
+    ) = block(
+        frame_lengths,
+        (
+            text_mask,
+            frames[0],
+            cotangent[0],
+            text[0],
+            cross_gain[None],
+            mod,
+            time,
+            vector,
+            qkv,
+            attended,
+            stats,
+        ),
+        (
+            w_attn_out,
+            w_cross_query,
+            w_cross_key,
+            w_cross_value,
+            w_cross_out,
+            w_mlp_in,
+            w_mlp_out,
+            w_query,
+            w_key,
+            w_value,
+            w_adaln,
+            w_time_out,
+        ),
+    )
+    (
+        block_out,
+        grad_frames,
+        grad_text,
+        sum_time_in,
+        sum_time_out,
+        sum_adaln,
+        sum_gain,
+        sum_mlp_in,
+        sum_mlp_out,
+        sum_cross_out,
+        sum_cross_query,
+        sum_attn_out,
+        sum_cross_key,
+        sum_cross_value,
+        sum_query,
+        sum_key,
+        sum_value,
+    ) = finish(
+        (
+            pieces,
+            block_out,
+            grad_frames,
+            grad_text,
+            gain_sum,
+            conditions,
+            hiddens,
+            vectors,
+            grad_mods,
+            grad_time_outs,
+            grad_time_firsts,
+        )
+    )
+    return (
+        block_out[None],
+        grad_frames[None],
+        grad_text[None],
+        sum_time_in.T,
+        sum_time_out.T,
+        sum_adaln.T,
+        sum_query.T,
+        sum_key.T,
+        sum_value.T,
+        sum_attn_out.T,
+        sum_gain[0],
+        sum_cross_query.T,
+        sum_cross_key.T,
+        sum_cross_value.T,
+        sum_cross_out.T,
+        sum_mlp_in,
+        sum_mlp_out.T,
+    )
+
+
+def on_device_general(
     frames,
     text,
     timesteps,
@@ -466,8 +1681,9 @@
         P(),
         P(),
     )
+    paired = mesh.shape["band"] == 4 and mesh.shape["seq"] == 8
     return jax.shard_map(
-        on_device,
+        on_device if paired else on_device_general,
         mesh=mesh,
         in_specs=placed,
         out_specs=(

time: 1410 us -> 201 us (0.14)
  waiting for transfers between devices: 846 us -> 0 us
  blocking collectives: 311 us -> 0 us
  Pallas kernels: 0 us -> 196 us
  matrix products: 112 us -> 0 us
  other arithmetic: 67.3 us -> 0.06 us
  local copies, waits for them, and re-layouts: 44.2 us -> 1.87 us
  between operations: 18.4 us -> 2.14 us
    reduce_scatter x11 -> x0, waiting for transfers between devices: 745 us -> none  [the longest x1 163 us: on_device(): lax.psum_scatter(grad_w_mlp_out, 'seq', scatter_dimension=1, tiled=True)]
    unnamed x1 -> x0, blocking collectives: 296 us -> none
    pallas_call x0 -> x3, Pallas kernels: none -> 196 us  [the longest x1 156 us: block(): pl.pallas_call(block_kernel, out_shape=(shape((128, D), bf16), shape((128...]
    dot_general x55 -> x0, matrix products: 112 us -> none  [the longest x10 29.5 us: transposed_left(): lax.dot_general(left, right, (((0,), (0,)), ((), ())), preferred_element_...]
    all_gather x1 -> x0, waiting for transfers between devices: 53 us -> none  [on_device(): lax.all_gather(kv_local, 'seq', axis=1, tiled=True)]
    psum x1 -> x0, waiting for transfers between devices: 47.8 us -> none  [on_device(): lax.psum(for_sending(shared + replicated), 'band')]
    convert_element_type x32 -> x0, other arithmetic: 40.8 us -> none  [the longest x13 20.6 us: for_sending(): a.astype(jnp.bfloat16)]
    psum x1 -> x0, blocking collectives: 15 us -> none  [on_device(): lax.psum(for_sending(shared + replicated), 'band')]
  transfers between devices with their start and end apart: 13 -> 0, of which waited for: 11 -> 0; matrix products, arithmetic and copies ran while one was open for 8% -> 0% of each run, Pallas kernels for 0% -> 0%
where the time goes in v2:
time: 201 us; the launch traced here: 200 us
  Pallas kernels  196 us (98%)
  between operations  2.14 us (1%)
    pallas_call x1, Pallas kernels, block(): pl.pallas_call(block_kernel, out_shape=(shape((128, D), bf16), shape((128...  156 us
    pallas_call x1, Pallas kernels, attend(): pl.pallas_call(attend_kernel, out_shape=(jax.ShapeDtypeStruct((8, 6 * D),...  34.9 us
    pallas_call x1, Pallas kernels, finish(): pl.pallas_call(final_kernel, out_shape=tuple((jax.ShapeDtypeStruct(*shape...  5.65 us

profile of v2, /device:TPU:0, one launch (start us, length us, event | category | flops | bytes accessed | tf_op | source)
XLA Modules:
  0.0 200.3 jit_solution(4212183589963762371)
XLA Ops:
  1.9 0.1 sine_convert_fusion
  2.0 1.3 broadcast_in_dim.19.refs_4_
  3.3 0.6 broadcast_in_dim.20.vector_ref.refs_7_
  3.9 34.9 %shard_map.323 = (f32[8,4608]{1,0:T(8,128)}, f32[8,1536]{1,0:T(8,128)}, bf16[3,8,128,768]{3,2,1,0:T(8,128)(2,1)}, f32[128,768]{1,0:T(8,128)}, f32[128,128]{1,0:T(8,128)}) custom-call(s32[1]{0:T(128)S(6)} %copy.38.length_ref, bf16[16,256]{1,0:T(8,128)(2,1)} %broadcast_in_dim.20.vector_ref.refs_7_, bf16[128,768]{1,0:T(8,128)(2,1)} %bitcast.20, ...), custom_call_target="tpu_custom_call" | custom-call | tf_op jit(solution)/shard_map/pallas_call | solution.py:405
  38.8 155.6 %shard_map.324 = (bf16[128,768]{1,0:T(8,128)(2,1)}, bf16[128,768]{1,0:T(8,128)(2,1)}, f32[16,768]{1,0:T(8,128)}, f32[8,768]{1,0:T(8,128)}, bf16[16,768]{1,0:T(8,...) custom-call(s32[1]{0:T(128)S(6)} %copy.38.length_ref, ...), custom_call_target="tpu_custom_call" | custom-call | tf_op jit(solution)/shard_map/pallas_call | solution.py:1103
  194.5 5.7 %shard_map.325 = (bf16[128,768]{1,0:T(8,128)(2,1)}, bf16[128,768]{1,0:T(8,128)(2,1)}, f32[16,768]{1,0:T(8,128)}, f32[96,256]{1,0:T(8,128)}, f32[96,768]{1,0:T(8,...) custom-call(bf16[16,2,2,48,384]{4,3,2,1,0:T(8,128)(2,1)} %get-tuple-, ...), custom_call_target="tpu_custom_call" | custom-call | tf_op jit(solution)/shard_map/pallas_call | solution.py:1212
  (1 shorter events, 0.0 us)

commit v3 on v2

--- a/solution.py
+++ b/solution.py
@@ -269,167 +269,8 @@
     return jnp.where(head_mask(half), tile, jnp.zeros_like(tile))
 
 
-def attend_kernel(
-    length_ref,
-    vector_ref,
-    frames_ref,
-    w_time_in_ref,
-    w_time_out_ref,
-    w_adaln_ref,
-    w_query_ref,
-    w_key_ref,
-    w_value_ref,
-    mod_ref,
-    time_ref,
-    qkv_ref,
-    attended_ref,
-    stats_ref,
-    gathered,
-    time_in,
-    time_out,
-    adaln,
-    projections,
-    load_sems,
-    recv,
-    up,
-    down,
-    across,
-):
-    y, core, z, x = places()
-    me = z * 2 + x
-    own = pltpu.make_async_copy(frames_ref, gathered.at[me], load_sems.at[0])
-    own.start()
-    loads = [
-        pltpu.make_async_copy(w_time_in_ref, time_in, load_sems.at[1]),
-        pltpu.make_async_copy(w_time_out_ref, time_out, load_sems.at[2]),
-    ]
-    loads += [
-        pltpu.make_async_copy(
-            w_adaln_ref.at[:, pl.ds(i * 1536, 1536)], adaln.at[i], load_sems.at[3 + i]
-        )
-        for i in range(3)
-    ]
-    loads += [
-        pltpu.make_async_copy(ref, projections.at[i], load_sems.at[6 + i])
-        for i, ref in enumerate((w_query_ref, w_key_ref, w_value_ref))
-    ]
-    for load in loads:
-        load.start()
-    neighbours = Spread([gathered], recv, up, down, across)
-    barrier = pltpu.get_barrier_semaphore()
-    pl.semaphore_signal(
-        barrier, inc=1, device_id=device(y, core, z, 1 - x), device_id_type=MESH
-    )
-
-    @pl.when(z < 3)
-    def _():
-        pl.semaphore_signal(barrier, inc=1, device_id=device(y, core, z + 1, x), device_id_type=MESH)
-
-    @pl.when(z > 0)
-    def _():
-        pl.semaphore_signal(barrier, inc=1, device_id=device(y, core, z - 1, x), device_id_type=MESH)
-
-    pl.semaphore_wait(barrier, 2 + lax.rem(lax.div(z + 1, 2), 2))
-    own.wait()
-    neighbours.start()
-    loads[0].wait()
-    first = product(vector_ref[...], time_in[...])
-    hidden = narrow(silu(first))
-    loads[1].wait()
-    second = product(hidden, time_out[...])
-    condition = narrow(silu(second))
-    time_ref[:, 0:D] = first[0:8]
-    time_ref[:, D : 2 * D] = second[0:8]
-    loads[2].wait()
-    mod_ref[:, 0:1536] = product(condition, adaln[0])[0:8]
-    neighbours.relay(1)
-    loads[3].wait()
-    mod_ref[:, 1536:3072] = product(condition, adaln[1])[0:8]
-    neighbours.relay(2)
-    loads[4].wait()
-    mod_ref[:, 3072:4608] = product(condition, adaln[2])[0:8]
-    neighbours.relay(3)
-    for load in loads[5:]:
-        load.wait()
-
-    def project(slot):
-        normed, unused = layer_norm(gathered[slot].astype(jnp.float32))
-        low = narrow(normed * (1.0 + mod_ref[0:1, D : 2 * D]) + mod_ref[0:1, 0:D])
-        for i in range(3):
-            qkv_ref[i, slot] = narrow(product(low, projections[i]))
-
-    def own_column(row, unused):
-        project(row * 2 + x)
-        return unused
-
-    def other_column(row, unused):
-        neighbours.arrived(row * 2 + 1 - x)
-        project(row * 2 + 1 - x)
-        return unused
-
-    lax.fori_loop(0, 4, own_column, 0)
-    lax.fori_loop(0, 4, other_column, 0)
-    length = length_ref[0]
-    key_valid = lax.broadcasted_iota(jnp.int32, (1, 1024), 1) < length
-    lane = lax.broadcasted_iota(jnp.int32, (1, 128), 1)
-
-    def pair(tile, stats):
-        at = pl.ds(pl.multiple_of(tile * 128, 128), 128)
-        query = qkv_ref[0, me, :, at]
-        keys = qkv_ref[1, :, :, at].reshape(1024, 128)
-        values = qkv_ref[2, :, :, at].reshape(1024, 128)
-        outs = []
-        for half in range(2):
-            scores = transposed_right(keep_head(query, half), keys) * 0.125
-            scores = jnp.where(key_valid, scores, masked_value)
-            row_max = jnp.max(scores, axis=1, keepdims=True)
-            expanded = jnp.exp(scores - row_max)
-            row_sum = jnp.sum(expanded, axis=1, keepdims=True)
-            outs.append(product(narrow(expanded), values) / row_sum)
-            stats = jnp.where(lane == tile * 2 + half, row_max + jnp.log(row_sum), stats)
-        attended_ref[:, at] = jnp.where(head_mask(0), outs[0], outs[1])
-        return stats
-
-    stats_ref[...] = lax.fori_loop(0, 6, pair, jnp.zeros((128, 128), jnp.float32))
-    neighbours.finish()
-
-
 def vmem(*shape, dtype=jnp.bfloat16):
     return pltpu.VMEM(shape, dtype)
-
-
-def attend(length, vector, frames, weights):
-    dma = pltpu.SemaphoreType.DMA
-    in_vmem = pl.BlockSpec(memory_space=pltpu.VMEM)
-    in_place = pl.BlockSpec(memory_space=pl.ANY)
-    return pl.pallas_call(
-        attend_kernel,
-        out_shape=(
-            jax.ShapeDtypeStruct((8, 6 * D), jnp.float32),
-            jax.ShapeDtypeStruct((8, 2 * D), jnp.float32),
-            jax.ShapeDtypeStruct((3, 8, 128, D), jnp.bfloat16),
-            jax.ShapeDtypeStruct((128, D), jnp.float32),
-            jax.ShapeDtypeStruct((128, 128), jnp.float32),
-        ),
-        in_specs=[pl.BlockSpec(memory_space=pltpu.SMEM), in_vmem] + [in_place] * 7,
-        out_specs=(in_vmem,) * 5,
-        scratch_shapes=[
-            vmem(8, 128, D),
-            vmem(256, D),
-            vmem(D, D),
-            vmem(3, D, 1536),
-            vmem(3, D, D),
-            dma((9,)),
-            dma((1, 8)),
-            dma((1, 4)),
-            dma((1, 4)),
-            dma((1, 4)),
-        ],
-        compiler_params=pltpu.CompilerParams(
-            collective_id=1, has_side_effects=True, vmem_limit_bytes=VMEM_BYTES
-        ),
-    )(length, vector, frames, *weights)
-
 
 PRODUCTS = (
     [(1 + j, 4) for j in range(4)]
@@ -437,7 +278,7 @@
     + [(5, 5), (6, 6), (9, 8), (9, 9), (7, 7)]
     + [(8, 10), (8, 11), (8, 12)]
 )
-LEFTS = 9
+LEFTS = 8
 RIGHTS = 13
 TEXT_UNIT = 9
 SLOTS = 4
@@ -448,12 +289,7 @@
     "cotangent",
     "text",
     "gain",
-    "mod",
-    "time",
     "vector",
-    "qkv",
-    "attended",
-    "stats",
 ]
 IN_PLACE = [
     "hbm_out",
@@ -468,6 +304,7 @@
     "hbm_value",
     "hbm_adaln",
     "hbm_time_out",
+    "hbm_time_in",
 ]
 OUT_VMEM = [
     "block_out",
@@ -489,6 +326,18 @@
     sem = lambda *shape: pltpu.SemaphoreType.DMA(shape)
     f32 = jnp.float32
     return dict(
+        mod=vmem(8, 6 * D, dtype=f32),
+        time=vmem(8, 2 * D, dtype=f32),
+        qkv=vmem(3, 8, 128, D),
+        attended=vmem(128, D, dtype=f32),
+        pair=vmem(2, 128, D),
+        stats=vmem(128, 128, dtype=f32),
+        gathered=vmem(8, 128, D),
+        time_in=vmem(256, D),
+        fr_recv=sem(1, 8),
+        fr_up=sem(1, 4),
+        fr_down=sem(1, 4),
+        fr_across=sem(1, 4),
         square=vmem(9, D, D),
         mlp_in=vmem(D, 4 * D),
         mlp_out=vmem(4 * D, D),
@@ -547,13 +396,8 @@
         after=vmem(128, D, dtype=f32),
         pre=vmem(4, 128, D, dtype=f32),
         acc=vmem(128, D, dtype=f32),
-        grad_pre=vmem(4, 128, D),
         grad_mlp=vmem(128, D),
-        cross_q=vmem(128, D),
-        cross_k=vmem(128, D),
-        cross_v=vmem(128, D),
         cross_probs=vmem(12, 128, 128, dtype=f32),
-        grad_heads=vmem(128, D),
         grad_q=vmem(128, D),
         grad_k=vmem(128, D),
         grad_v=vmem(128, D),
@@ -582,6 +426,8 @@
         self.r = r
         self.y, self.core, self.z, self.x = y, core, z, x = places()
         self.across = device(y, core, z, 1 - x)
+        self.high, self.low = lax.div(z, 2), lax.rem(z, 2)
+        self.along = device(y, core, 2 * self.high + 1 - self.low, x)
         self.clips = [
             None,
             device(y, 1 - core, z, x),
@@ -592,11 +438,16 @@
 
     def left_copy(self, u):
         r = self.r
-        return remote(r.lefts.at[u], r.lrecv.at[u], r.ls.at[u], r.lr.at[u], self.across)
+        to = self.along if 1 <= u <= 4 else self.across
+        return remote(r.lefts.at[u], r.lrecv.at[u], r.ls.at[u], r.lr.at[u], to)
 
     def right_copy(self, u):
         r = self.r
-        return remote(r.gt.at[u, 1 - self.x], r.grecv.at[u], r.gs.at[u], r.gr.at[u], self.across)
+        if u == 4:
+            half, to = 1 - self.low, self.along
+        else:
+            half, to = 1 - self.x, self.across
+        return remote(r.gt.at[u, half], r.grecv.at[u], r.gs.at[u], r.gr.at[u], to)
 
     def core_copy(self, i):
         r = self.r
@@ -608,15 +459,18 @@
         mine = r.qbuf.at[i % SLOTS, 1 - self.y]
         return remote(mine, r.qrecv.at[i], r.qs.at[i], r.qr.at[i], self.clips[2])
 
+    def spot(self, i):
+        return self.high * 2 + self.x if 1 <= PRODUCTS[i][0] <= 4 else self.z
+
     def z_copy(self, i, k):
         r = self.r
-        to = lax.rem(self.z + k, 4)
+        to = lax.rem(self.spot(i) + k, 4)
+        if 1 <= PRODUCTS[i][0] <= 4:
+            target = device(self.y, self.core, 2 * lax.div(to, 2) + self.low, lax.rem(to, 2))
+        else:
+            target = device(self.y, self.core, to, self.x)
         return remote(
-            r.rbuf.at[i % SLOTS, to],
-            r.rrecv.at[i, k],
-            r.rs.at[i, k],
-            r.rr.at[i, k],
-            device(self.y, self.core, to, self.x),
+            r.rbuf.at[i % SLOTS, to], r.rrecv.at[i, k], r.rs.at[i, k], r.rr.at[i, k], target
         )
 
     def last_y_copy(self, i):
@@ -642,27 +496,28 @@
         for s in range(8):
             for c in range(2):
                 at = s * 96 + c * PART
-                self.r.gt[u, s % 2, c, pl.ds((s // 2) * PART, PART), :] = turned[at : at + PART]
+                half, block = (s // 2 % 2, s // 4 * 2 + s % 2) if u == 4 else (s % 2, s // 2)
+                self.r.gt[u, half, c, pl.ds(block * PART, PART), :] = turned[at : at + PART]
         self.right_copy(u).start()
 
     def multiply(self, i):
-        r, x = self.r, self.x
+        r = self.r
         left, right = PRODUCTS[i]
-        if left != TEXT_UNIT and (i == 0 or PRODUCTS[i - 1][0] != left):
+        if left < LEFTS and (i == 0 or PRODUCTS[i - 1][0] != left):
             self.left_copy(left).wait_recv()
         if i == 0 or PRODUCTS[i - 1][1] != right:
             self.right_copy(right).wait_recv()
         if i >= SLOTS:
             self.core_copy(i - SLOTS).wait_send()
         for c in range(2):
-            mine, theirs = r.gt[right, x, c], r.grecv[right, c]
+            mine, theirs = r.gt[right, self.low if right == 4 else self.x, c], r.grecv[right, c]
             if left == TEXT_UNIT:
                 both = narrow(mine.astype(jnp.float32) + theirs.astype(jnp.float32))
                 part = product(both, r.text[...])
             else:
+                both = (r.pair[0], r.pair[1]) if left == 8 else (r.lefts[left], r.lrecv[left])
                 part = product(
-                    jnp.concatenate([mine, theirs], axis=1),
-                    jnp.concatenate([r.lefts[left], r.lrecv[left]], axis=0),
+                    jnp.concatenate([mine, theirs], axis=1), jnp.concatenate(both, axis=0)
                 )
             r.pbuf[i % SLOTS, c] = narrow(part)
         self.core_copy(i).start()
@@ -697,7 +552,7 @@
         r = self.r
         for k in (1, 2, 3):
             self.z_copy(i, k).wait_recv()
-        total = r.rbuf[i % SLOTS, self.z].astype(jnp.float32)
+        total = r.rbuf[i % SLOTS, self.spot(i)].astype(jnp.float32)
         for k in (1, 2, 3):
             total = total + r.rrecv[i, k].astype(jnp.float32)
         r.final[i, self.core, self.y] = narrow(total)
@@ -752,6 +607,7 @@
     y, core, z, x = places()
     me, band = z * 2 + x, y * 2 + core
     peers = [device(y, core, lax.div(s, 2), lax.rem(s, 2)) for s in [lax.rem(me + k, 8) for k in range(8)]]
+    r.cross_q, r.cross_k, r.cross_v, r.grad_heads = [r.gathered.at[i] for i in range(4, 8)]
     sums = Sums(r)
 
     def load(i, src, dst):
@@ -774,9 +630,18 @@
     loads.append(load(10, r.hbm_mlp_out, r.mlp_out))
     loads.append(load(11, r.hbm_adaln.at[:, pl.ds(3072, 1536)], r.adaln_high))
     adaln_low = load(12, r.hbm_adaln.at[:, pl.ds(0, 3072)], r.mlp_in)
-    for i in (0, 2, 3, 1, 4, 9, 10, 5, 6, 7, 8, 11):
+    load_time_in = load(13, r.hbm_time_in, r.time_in)
+    own_frames = load(14, r.frames, r.gathered.at[me])
+    own_frames.start()
+    load_time_in.start()
+    loads[TIME].start()
+    adaln_low.start()
+    for i in (11, WQ, WK, WV, OUT, CK, CV, CQ, CO, 10):
         loads[i].start()
     greet(peers[1:] + sums.clips[1:])
+    own_frames.wait()
+    neighbours = Spread([r.gathered], r.fr_recv, r.fr_up, r.fr_down, r.fr_across)
+    neighbours.start()
 
     def clip_copy(refs, sems, recvs, j):
         return [
@@ -784,32 +649,98 @@
             for i, ref in enumerate(refs)
         ]
 
+    length = length_ref[0]
+
+    def row_valid():
+        return lax.broadcasted_iota(jnp.int32, (128, 1), 0) + me * 128 < length
+
+    def modulation(i):
+        return r.mod[0:1, i * D : (i + 1) * D]
+
+    def over_rows(values):
+        return jnp.sum(values, axis=0, keepdims=True)
+
+    lane = lax.broadcasted_iota(jnp.int32, (1, 128), 1)
+    text_valid = r.mask[...] != 0
+    gain = r.gain[...].astype(jnp.float32)
+
+    def tile_at(tile):
+        return pl.ds(pl.multiple_of(tile * 128, 128), 128)
+
+    load_time_in.wait()
+    first = product(r.vector[...], r.time_in[...])
+    hidden = narrow(silu(first))
+    loads[TIME].wait()
+    second = product(hidden, r.square[TIME])
+    condition = narrow(silu(second))
+    r.time[:, 0:D] = first[0:8]
+    r.time[:, D : 2 * D] = second[0:8]
     r.times[band] = r.time[...]
     r.vecs[band] = r.vector[...]
     for j in (1, 2, 3):
         for copy in clip_copy((r.times, r.vecs), r.ts, r.tr, j):
             copy.start()
 
-    length = length_ref[0]
-
-    def row_valid():
-        return lax.broadcasted_iota(jnp.int32, (128, 1), 0) + me * 128 < length
-
-    def modulation(i):
-        return r.mod[0:1, i * D : (i + 1) * D]
-
-    def over_rows(values):
-        return jnp.sum(values, axis=0, keepdims=True)
-
-    lane = lax.broadcasted_iota(jnp.int32, (1, 128), 1)
-    text_valid = r.mask[...] != 0
-    gain = r.gain[...].astype(jnp.float32)
-
-    def tile_at(tile):
-        return pl.ds(pl.multiple_of(tile * 128, 128), 128)
-
-    normed, unused = layer_norm(r.frames[...].astype(jnp.float32))
-    sums.post_left(8, narrow(normed * (1.0 + modulation(1)) + modulation(0)))
+    adaln_low.wait()
+    r.mod[:, 0:1536] = product(condition, r.mlp_in[:, 0:1536])[0:8]
+    neighbours.relay(1)
+    r.mod[:, 1536:3072] = product(condition, r.mlp_in[:, 1536:3072])[0:8]
+    loads[9].start()
+    loads[11].wait()
+    r.mod[:, 3072:4608] = product(condition, r.adaln_high[...])[0:8]
+    for i in (WQ, WK, WV):
+        loads[i].wait()
+    def project(row, column):
+        normed, unused = layer_norm(r.gathered[row * 2 + column].astype(jnp.float32))
+        low = narrow(normed * (1.0 + modulation(1)) + modulation(0))
+        for i in range(3):
+            r.qkv[i, row * 2 + column] = narrow(product(low, r.square[WQ + i]))
+        return low
+
+    def own_column(row, unused):
+        low = project(row, x)
+
+        @pl.when(row == z)
+        def _():
+            r.pair[0] = low
+
+        return unused
+
+    def other_column(row, unused):
+        neighbours.arrived(row * 2 + 1 - x)
+        low = project(row, 1 - x)
+
+        @pl.when(row == z)
+        def _():
+            r.pair[1] = low
+
+        return unused
+
+    neighbours.relay(2)
+    neighbours.relay(3)
+    lax.fori_loop(0, 4, own_column, 0)
+    lax.fori_loop(0, 4, other_column, 0)
+    key_valid = lax.broadcasted_iota(jnp.int32, (1, 1024), 1) < length
+
+    def attend_pair(tile, stats):
+        at = tile_at(tile)
+        query = r.qkv[0, me, :, at]
+        keys = r.qkv[1, :, :, at].reshape(1024, 128)
+        values = r.qkv[2, :, :, at].reshape(1024, 128)
+        outs = []
+        for half in range(2):
+            scores = transposed_right(keep_head(query, half), keys) * 0.125
+            scores = jnp.where(key_valid, scores, masked_value)
+            row_max = jnp.max(scores, axis=1, keepdims=True)
+            expanded = jnp.exp(scores - row_max)
+            row_sum = jnp.sum(expanded, axis=1, keepdims=True)
+            outs.append(product(narrow(expanded), values) / row_sum)
+            stats = jnp.where(lane == tile * 2 + half, row_max + jnp.log(row_sum), stats)
+        r.attended[:, at] = jnp.where(head_mask(0), outs[0], outs[1])
+        return stats
+
+    r.stats[...] = lax.fori_loop(0, 6, attend_pair, jnp.zeros((128, 128), jnp.float32))
+    neighbours.finish()
     sums.post_left(7, narrow(r.attended[...]))
     r.grad_mlp[...] = narrow(
         modulation(5) * jnp.where(row_valid(), r.cotangent[...].astype(jnp.float32), 0.0)
@@ -867,7 +798,7 @@
     for j in range(4):
         slope = gelu_slope(r.pre[j])
         grad = narrow(slope * transposed_right(r.grad_mlp[...], r.mlp_out[j * D : (j + 1) * D, :]))
-        r.grad_pre[j] = grad
+        r.gathered[j] = grad
         for part in range(2):
             s = j * 2 + part
             turned = narrow(
@@ -879,10 +810,12 @@
                     r.gt[u, s % 2, c, pl.ds((s // 2) * PART, PART), :] = turned[at : at + PART]
     for u in range(4):
         sums.right_copy(u).start()
+    sums.step(1)
     for j in range(4):
-        part = transposed_right(r.grad_pre[j], r.mlp_in[:, j * D : (j + 1) * D])
+        part = transposed_right(r.gathered[j], r.mlp_in[:, j * D : (j + 1) * D])
         r.acc[...] = part if j == 0 else r.acc[...] + part
     adaln_low.start()
+    sums.step(2)
     r.sums[3:4, :] = over_rows(r.acc[...])
     r.sums[4:5, :] = over_rows(r.acc[...] * r.normed_mlp[...])
     grad_res = jnp.where(row_valid(), r.cotangent[...].astype(jnp.float32), 0.0)
@@ -918,6 +851,7 @@
 
     lax.fori_loop(0, 6, cross_pair_back, 0)
     sums.post_right(6, r.grad_q[...])
+    sums.step(2)
     grad_cross_in = transposed_right(r.grad_q[...], r.square[CQ])
     r.sums[6:7, :] = over_rows(grad_cross_in * r.normed_cross[...])
     r.sums[7:8, :] = jnp.zeros((1, D), jnp.float32)
@@ -939,6 +873,7 @@
     spread = Spread([r.heads, r.rowstats], r.sp_recv, r.sp_up, r.sp_down, r.sp_across)
     spread.start()
     sums.post_right(7, low)
+    sums.step(1)
     r.sums[2:3, :] = over_rows(r.middle[...] * r.proj[...])
     sums.post_right(8, r.grad_k[...])
     sums.post_right(9, r.grad_v[...])
@@ -957,6 +892,7 @@
     for k in range(1, 8):
         text_copy(k).start()
     spread.relay(1)
+    sums.step(1)
     key_valid = lax.broadcasted_iota(jnp.int32, (1, 1024), 1) < length
 
     def query_pair(tile, unused):
@@ -980,11 +916,13 @@
 
     lax.fori_loop(0, 2, query_pair, 0)
     spread.relay(2)
+    sums.step(1)
     lax.fori_loop(2, 4, query_pair, 0)
     spread.relay(3)
+    sums.step(1)
     lax.fori_loop(4, 6, query_pair, 0)
     sums.post_right(10, r.grad_q[...])
-    sums.step(6)
+    sums.step(3)
     for row in range(4):
         spread.arrived(row * 2 + 1 - x)
 
@@ -1012,8 +950,7 @@
     lax.fori_loop(0, 6, key_pair, 0)
     sums.post_right(11, r.grad_k[...])
     sums.post_right(12, r.grad_v[...])
-    for i in (WQ, WK, WV):
-        loads[i].wait()
+    sums.step(1)
     grad_in = (
         transposed_right(r.grad_q[...], r.square[WQ])
         + transposed_right(r.grad_k[...], r.square[WK])
@@ -1029,11 +966,11 @@
 
     for k in range(1, 8):
         sums_copy(k).start()
+    sums.step(3)
     grads = r.middle[...] + norm_back(normed, scaling, r.acc[...] * (1.0 + modulation(1)))
     r.grad_frames[...] = narrow(
         jnp.where(row_valid(), grads, r.cotangent[...].astype(jnp.float32))
     )
-    sums.step(4)
     total = r.sums[...]
     for k in range(1, 8):
         sums_copy(k).wait_recv()
@@ -1047,7 +984,7 @@
 
     for j in (1, 2, 3):
         total_copy(j).start()
-    sums.step(3)
+    sums.step(2)
     for j in (1, 2, 3):
         total_copy(j).wait_recv()
         for copy in clip_copy((r.times, r.vecs), r.ts, r.tr, j):
@@ -1071,8 +1008,6 @@
     for b in range(4):
         r.vectors[b] = r.vecs[b]
     adaln_low.wait()
-    loads[11].wait()
-    loads[TIME].wait()
     grad_condition = transposed_right(r.grad_mods[:, :3072], r.mlp_in[...]) + transposed_right(
         r.grad_mods[:, 3072:], r.adaln_high[...]
     )
@@ -1247,12 +1182,6 @@
     w_mlp_out,
 ):
     vector = jnp.broadcast_to(narrow(time_embed(timesteps, w_time_in.shape[0])), (16, 256))
-    mod, time, qkv, attended, stats = attend(
-        frame_lengths,
-        vector,
-        frames[0],
-        (w_time_in, w_time_out, w_adaln, w_query, w_key, w_value),
-    )
     (
         block_out,
         grad_frames,
@@ -1273,12 +1202,7 @@
             cotangent[0],
             text[0],
             cross_gain[None],
-            mod,
-            time,
             vector,
-            qkv,
-            attended,
-            stats,
         ),
         (
             w_attn_out,
@@ -1293,6 +1217,7 @@
             w_value,
             w_adaln,
             w_time_out,
+            w_time_in,
         ),
     )
     (

time: 201 us -> 161 us (0.80)
  Pallas kernels: 196 us -> 156 us
    pallas_call x1 -> x0, Pallas kernels: 34.9 us -> none  [attend(): pl.pallas_call(attend_kernel, out_shape=(jax.ShapeDtypeStruct((8, 6 * D),...]
    pallas_call x1, Pallas kernels: 156 us -> 150 us  [block(): pl.pallas_call(block_kernel, out_shape=(shape((128, D), bf16), shape((128...]
where the time goes in v3:
time: 161 us; the launch traced here: 160 us
  Pallas kernels  156 us (97%)
  between operations  2.15 us (1%)
  local copies, waits for them, and re-layouts  1.87 us (1%)
    pallas_call x1, Pallas kernels, block(): pl.pallas_call(block_kernel, out_shape=(shape((128, D), bf16), shape((128...  150 us
    pallas_call x1, Pallas kernels, finish(): pl.pallas_call(final_kernel, out_shape=tuple((jax.ShapeDtypeStruct(*shape...  5.65 us

profile of v3, /device:TPU:0, one launch (start us, length us, event | category | flops | bytes accessed | tf_op | source)
XLA Modules:
  0.0 159.8 jit_solution(16171165550435652998)
XLA Ops:
  1.9 0.1 sine_convert_fusion
  2.0 1.3 broadcast_in_dim.19.refs_4_
  3.3 0.6 broadcast_in_dim.20.refs_5_
  3.9 150.1 %shard_map.323 = (bf16[128,768]{1,0:T(8,128)(2,1)}, bf16[128,768]{1,0:T(8,128)(2,1)}, f32[16,768]{1,0:T(8,128)}, f32[8,768]{1,0:T(8,128)}, bf16[16,768]{1,0:T(8,...) custom-call(s32[1]{0:T(128)S(6)} %copy.38.length_ref, ...), custom_call_target="tpu_custom_call" | custom-call | tf_op jit(solution)/shard_map/pallas_call | solution.py:1038
  154.0 5.7 %shard_map.324 = (bf16[128,768]{1,0:T(8,128)(2,1)}, bf16[128,768]{1,0:T(8,128)(2,1)}, f32[16,768]{1,0:T(8,128)}, f32[96,256]{1,0:T(8,128)}, f32[96,768]{1,0:T(8,...) custom-call(bf16[16,2,2,48,384]{4,3,2,1,0:T(8,128)(2,1)} %get-tuple-, ...), custom_call_target="tpu_custom_call" | custom-call | tf_op jit(solution)/shard_map/pallas_call | solution.py:1147
  (1 shorter events, 0.0 us)

commit v4 on v3

--- a/solution.py
+++ b/solution.py
@@ -166,94 +166,107 @@
 
 
 class Spread:
-    def __init__(self, buffers, recv, up, down, across):
-        self.buffers, self.recv, self.up, self.down, self.across = buffers, recv, up, down, across
+    def __init__(self, chunks, recv, up, down, across):
+        self.chunks, self.recv, self.up, self.down, self.across = chunks, recv, up, down, across
         self.y, self.core, self.z, self.x = places()
 
-    def copies(self, slot, sems, at, target):
+    def copies(self, chunk, slot, sems, at, target):
+        first = sum(len(pieces) for pieces in self.chunks[:chunk])
         return [
-            remote(buf.at[slot], buf.at[slot], sems.at[i, at], self.recv.at[i, slot], target)
-            for i, buf in enumerate(self.buffers)
+            remote(
+                piece(slot),
+                piece(slot),
+                sems.at[first + i, at],
+                self.recv.at[first + i, slot],
+                target,
+            )
+            for i, piece in enumerate(self.chunks[chunk])
         ]
 
-    def to_up(self, k):
-        return self.copies(
-            (self.z - k) * 2 + self.x, self.up, k, device(self.y, self.core, self.z + 1, self.x)
-        )
-
-    def to_down(self, k):
-        return self.copies(
-            (self.z + k) * 2 + self.x, self.down, k, device(self.y, self.core, self.z - 1, self.x)
-        )
-
-    def to_across(self, row):
-        return self.copies(
-            row * 2 + self.x, self.across, row, device(self.y, self.core, self.z, 1 - self.x)
-        )
-
-    def arrived(self, slot):
-        for copy in self.copies(slot, self.across, 0, device(self.y, self.core, self.z, 1 - self.x)):
+    def to_up(self, chunk, k):
+        slot = (self.z - k) * 2 + self.x
+        target = device(self.y, self.core, self.z + 1, self.x)
+        return self.copies(chunk, slot, self.up, k, target)
+
+    def to_down(self, chunk, k):
+        slot = (self.z + k) * 2 + self.x
+        target = device(self.y, self.core, self.z - 1, self.x)
+        return self.copies(chunk, slot, self.down, k, target)
+
+    def to_across(self, chunk, row):
+        target = device(self.y, self.core, self.z, 1 - self.x)
+        return self.copies(chunk, row * 2 + self.x, self.across, row, target)
+
+    def arrived(self, chunk, slot):
+        target = device(self.y, self.core, self.z, 1 - self.x)
+        for copy in self.copies(chunk, slot, self.across, 0, target):
             copy.wait_recv()
+
+    def all_arrived(self, slot):
+        for chunk in range(len(self.chunks)):
+            self.arrived(chunk, slot)
 
     def start(self):
         z = self.z
-
-        @pl.when(z < 3)
-        def _():
-            for copy in self.to_up(0):
+        for chunk in range(len(self.chunks)):
+
+            @pl.when(z < 3)
+            def _():
+                for copy in self.to_up(chunk, 0):
+                    copy.start()
+
+            @pl.when(z > 0)
+            def _():
+                for copy in self.to_down(chunk, 0):
+                    copy.start()
+
+            for copy in self.to_across(chunk, z):
                 copy.start()
 
-        @pl.when(z > 0)
-        def _():
-            for copy in self.to_down(0):
-                copy.start()
-
-        for copy in self.to_across(z):
-            copy.start()
-
-    def relay(self, k):
+    def relay(self, k, chunk):
         z = self.z
 
         @pl.when(z >= k)
         def _():
-            self.arrived((z - k) * 2 + self.x)
+            self.arrived(chunk, (z - k) * 2 + self.x)
 
             @pl.when(z < 3)
             def _():
-                for copy in self.to_up(k):
+                for copy in self.to_up(chunk, k):
                     copy.start()
 
-            for copy in self.to_across(z - k):
+            for copy in self.to_across(chunk, z - k):
                 copy.start()
 
         @pl.when(z + k <= 3)
         def _():
-            self.arrived((z + k) * 2 + self.x)
+            self.arrived(chunk, (z + k) * 2 + self.x)
 
             @pl.when(z > 0)
             def _():
-                for copy in self.to_down(k):
+                for copy in self.to_down(chunk, k):
                     copy.start()
 
-            for copy in self.to_across(z + k):
+            for copy in self.to_across(chunk, z + k):
                 copy.start()
 
     def finish(self):
         z = self.z
-        for k in range(4):
-
-            @pl.when((z >= k) & (z < 3))
-            def _():
-                for copy in self.to_up(k):
+        for chunk in range(len(self.chunks)):
+            for k in range(4):
+
+                @pl.when((z >= k) & (z < 3))
+                def _():
+                    for copy in self.to_up(chunk, k):
+                        copy.wait_send()
+
+                @pl.when((z + k <= 3) & (z > 0))
+                def _():
+                    for copy in self.to_down(chunk, k):
+                        copy.wait_send()
+
+                for copy in self.to_across(chunk, k):
                     copy.wait_send()
-
-            @pl.when((z + k <= 3) & (z > 0))
-            def _():
-                for copy in self.to_down(k):
-                    copy.wait_send()
-
-            for copy in self.to_across(k):
-                copy.wait_send()
 
 
 def silu(values):
@@ -273,8 +286,7 @@
     return pltpu.VMEM(shape, dtype)
 
 PRODUCTS = (
-    [(1 + j, 4) for j in range(4)]
-    + [(0, j) for j in range(4)]
+    [(1, 4), (0, 0), (2, 4), (0, 1), (0, 2), (3, 4), (0, 3), (4, 4)]
     + [(5, 5), (6, 6), (9, 8), (9, 9), (7, 7)]
     + [(8, 10), (8, 11), (8, 12)]
 )
@@ -282,7 +294,7 @@
 RIGHTS = 13
 TEXT_UNIT = 9
 SLOTS = 4
-LATER = (0, 1, 3, 5, 7, 8)
+LATER = (0, 1, 3, 7, 9, 10)
 IN_VMEM = [
     "mask",
     "frames",
@@ -334,10 +346,10 @@
         stats=vmem(128, 128, dtype=f32),
         gathered=vmem(8, 128, D),
         time_in=vmem(256, D),
-        fr_recv=sem(1, 8),
-        fr_up=sem(1, 4),
-        fr_down=sem(1, 4),
-        fr_across=sem(1, 4),
+        fr_recv=sem(2, 8),
+        fr_up=sem(2, 4),
+        fr_down=sem(2, 4),
+        fr_across=sem(2, 4),
         square=vmem(9, D, D),
         mlp_in=vmem(D, 4 * D),
         mlp_out=vmem(4 * D, D),
@@ -369,10 +381,10 @@
         out_sems=sem(n),
         heads=vmem(8, 128, D),
         rowstats=vmem(8, 32, 128, dtype=f32),
-        sp_recv=sem(2, 8),
-        sp_up=sem(2, 4),
-        sp_down=sem(2, 4),
-        sp_across=sem(2, 4),
+        sp_recv=sem(3, 8),
+        sp_up=sem(3, 4),
+        sp_down=sem(3, 4),
+        sp_across=sem(3, 4),
         times=vmem(4, 8, 2 * D, dtype=f32),
         vecs=vmem(4, 16, 256),
         ts=sem(2, 4),
@@ -503,9 +515,9 @@
     def multiply(self, i):
         r = self.r
         left, right = PRODUCTS[i]
-        if left < LEFTS and (i == 0 or PRODUCTS[i - 1][0] != left):
+        if left < LEFTS and left not in [l for l, unused in PRODUCTS[:i]]:
             self.left_copy(left).wait_recv()
-        if i == 0 or PRODUCTS[i - 1][1] != right:
+        if right not in [r for unused, r in PRODUCTS[:i]]:
             self.right_copy(right).wait_recv()
         if i >= SLOTS:
             self.core_copy(i - SLOTS).wait_send()
@@ -640,7 +652,12 @@
         loads[i].start()
     greet(peers[1:] + sums.clips[1:])
     own_frames.wait()
-    neighbours = Spread([r.gathered], r.fr_recv, r.fr_up, r.fr_down, r.fr_across)
+
+    def half(ref, i):
+        return lambda slot: ref.at[slot, i * 64 : (i + 1) * 64]
+
+    chunks = [[half(r.gathered, i)] for i in range(2)]
+    neighbours = Spread(chunks, r.fr_recv, r.fr_up, r.fr_down, r.fr_across)
     neighbours.start()
 
     def clip_copy(refs, sems, recvs, j):
@@ -683,9 +700,10 @@
 
     adaln_low.wait()
     r.mod[:, 0:1536] = product(condition, r.mlp_in[:, 0:1536])[0:8]
-    neighbours.relay(1)
+    neighbours.relay(1, 0)
     r.mod[:, 1536:3072] = product(condition, r.mlp_in[:, 1536:3072])[0:8]
     loads[9].start()
+    neighbours.relay(1, 1)
     loads[11].wait()
     r.mod[:, 3072:4608] = product(condition, r.adaln_high[...])[0:8]
     for i in (WQ, WK, WV):
@@ -707,7 +725,7 @@
         return unused
 
     def other_column(row, unused):
-        neighbours.arrived(row * 2 + 1 - x)
+        neighbours.all_arrived(row * 2 + 1 - x)
         low = project(row, 1 - x)
 
         @pl.when(row == z)
@@ -716,8 +734,9 @@
 
         return unused
 
-    neighbours.relay(2)
-    neighbours.relay(3)
+    for k in (2, 3):
+        for chunk in range(2):
+            neighbours.relay(k, chunk)
     lax.fori_loop(0, 4, own_column, 0)
     lax.fori_loop(0, 4, other_column, 0)
     key_valid = lax.broadcasted_iota(jnp.int32, (1, 1024), 1) < length
@@ -810,12 +829,11 @@
                     r.gt[u, s % 2, c, pl.ds((s // 2) * PART, PART), :] = turned[at : at + PART]
     for u in range(4):
         sums.right_copy(u).start()
-    sums.step(1)
     for j in range(4):
         part = transposed_right(r.gathered[j], r.mlp_in[:, j * D : (j + 1) * D])
         r.acc[...] = part if j == 0 else r.acc[...] + part
     adaln_low.start()
-    sums.step(2)
+    sums.step(1)
     r.sums[3:4, :] = over_rows(r.acc[...])
     r.sums[4:5, :] = over_rows(r.acc[...] * r.normed_mlp[...])
     grad_res = jnp.where(row_valid(), r.cotangent[...].astype(jnp.float32), 0.0)
@@ -851,7 +869,7 @@
 
     lax.fori_loop(0, 6, cross_pair_back, 0)
     sums.post_right(6, r.grad_q[...])
-    sums.step(2)
+    sums.step(1)
     grad_cross_in = transposed_right(r.grad_q[...], r.square[CQ])
     r.sums[6:7, :] = over_rows(grad_cross_in * r.normed_cross[...])
     r.sums[7:8, :] = jnp.zeros((1, D), jnp.float32)
@@ -870,10 +888,10 @@
     r.rowstats[me] = jnp.concatenate(
         [jnp.transpose(r.stats[...])[:16], jnp.transpose(delta)[:16]], axis=0
     )
-    spread = Spread([r.heads, r.rowstats], r.sp_recv, r.sp_up, r.sp_down, r.sp_across)
+    chunks = [[half(r.heads, 0), lambda slot: r.rowstats.at[slot]], [half(r.heads, 1)]]
+    spread = Spread(chunks, r.sp_recv, r.sp_up, r.sp_down, r.sp_across)
     spread.start()
     sums.post_right(7, low)
-    sums.step(1)
     r.sums[2:3, :] = over_rows(r.middle[...] * r.proj[...])
     sums.post_right(8, r.grad_k[...])
     sums.post_right(9, r.grad_v[...])
@@ -891,8 +909,8 @@
 
     for k in range(1, 8):
         text_copy(k).start()
-    spread.relay(1)
-    sums.step(1)
+    sums.step(2)
+    spread.relay(1, 0)
     key_valid = lax.broadcasted_iota(jnp.int32, (1, 1024), 1) < length
 
     def query_pair(tile, unused):
@@ -914,17 +932,21 @@
         r.grad_q[:, at] = narrow(jnp.where(head_mask(0), outs[0], outs[1]) * 0.125)
         return unused
 
-    lax.fori_loop(0, 2, query_pair, 0)
-    spread.relay(2)
-    sums.step(1)
-    lax.fori_loop(2, 4, query_pair, 0)
-    spread.relay(3)
-    sums.step(1)
+    lax.fori_loop(0, 1, query_pair, 0)
+    spread.relay(1, 1)
+    lax.fori_loop(1, 3, query_pair, 0)
+    sums.step(2)
+    spread.relay(2, 0)
+    lax.fori_loop(3, 4, query_pair, 0)
+    spread.relay(2, 1)
     lax.fori_loop(4, 6, query_pair, 0)
+    sums.step(3)
+    spread.relay(3, 0)
+    spread.relay(3, 1)
     sums.post_right(10, r.grad_q[...])
-    sums.step(3)
+    sums.step(4)
     for row in range(4):
-        spread.arrived(row * 2 + 1 - x)
+        spread.all_arrived(row * 2 + 1 - x)
 
     def key_pair(tile, unused):
         at = tile_at(tile)
@@ -1103,9 +1125,9 @@
             axis=0,
         ).astype(jnp.float32)
 
-    put(7, jnp.transpose(jnp.concatenate([whole(4 + j) for j in range(4)], axis=0)))
+    put(7, jnp.transpose(jnp.concatenate([whole(PRODUCTS.index((0, j))) for j in range(4)], axis=0)))
     for j in range(4):
-        staged[8][:, j * D : (j + 1) * D] = whole(j)
+        staged[8][:, j * D : (j + 1) * D] = whole(PRODUCTS.index((1 + j, 4)))
     copy(8).start()
     for j, p in enumerate(SQUARES):
         put(9 + j, whole(p))

time: 161 us -> 150 us (0.932)
  Pallas kernels: 156 us -> 145 us
    pallas_call x1, Pallas kernels: 150 us -> 139 us  [block(): pl.pallas_call(block_kernel, out_shape=(shape((128, D), bf16), shape((128...]
where the time goes in v4:
time: 150 us; the launch traced here: 149 us
  Pallas kernels  145 us (97%)
  between operations  2.15 us (1%)
  local copies, waits for them, and re-layouts  1.87 us (1%)
    pallas_call x1, Pallas kernels, block(): pl.pallas_call(block_kernel, out_shape=(shape((128, D), bf16), shape((128...  139 us
    pallas_call x1, Pallas kernels, finish(): pl.pallas_call(final_kernel, out_shape=tuple((jax.ShapeDtypeStruct(*shape...  5.65 us

profile of v4, /device:TPU:0, one launch (start us, length us, event | category | flops | bytes accessed | tf_op | source)
XLA Modules:
  0.0 148.9 jit_solution(3720140274065706784)
XLA Ops:
  1.9 0.1 sine_convert_fusion
  2.0 1.3 broadcast_in_dim.19.refs_4_
  3.3 0.6 broadcast_in_dim.20.refs_5_
  3.9 139.2 %shard_map.323 = (bf16[128,768]{1,0:T(8,128)(2,1)}, bf16[128,768]{1,0:T(8,128)(2,1)}, f32[16,768]{1,0:T(8,128)}, f32[8,768]{1,0:T(8,128)}, bf16[16,768]{1,0:T(8,...) custom-call(s32[1]{0:T(128)S(6)} %copy.38.length_ref, ...), custom_call_target="tpu_custom_call" | custom-call | tf_op jit(solution)/shard_map/pallas_call | solution.py:1060
  143.1 5.7 %shard_map.324 = (bf16[128,768]{1,0:T(8,128)(2,1)}, bf16[128,768]{1,0:T(8,128)(2,1)}, f32[16,768]{1,0:T(8,128)}, f32[96,256]{1,0:T(8,128)}, f32[96,768]{1,0:T(8,...) custom-call(bf16[16,2,2,48,384]{4,3,2,1,0:T(8,128)(2,1)} %get-tuple-, ...), custom_call_target="tpu_custom_call" | custom-call | tf_op jit(solution)/shard_map/pallas_call | solution.py:1169
  (1 shorter events, 0.0 us)

commit v5 on v4

--- a/solution.py
+++ b/solution.py
@@ -294,7 +294,7 @@
 RIGHTS = 13
 TEXT_UNIT = 9
 SLOTS = 4
-LATER = (0, 1, 3, 7, 9, 10)
+LATER = (0, 1, 3, 7, 10, 12)
 IN_VMEM = [
     "mask",
     "frames",

time: 150 us -> 149 us (level)
  no operation moved by 1% of the time
where the time goes in v5:
time: 149 us; the launch traced here: 148 us
  Pallas kernels  144 us (97%)
  between operations  2.15 us (1%)
  local copies, waits for them, and re-layouts  1.87 us (1%)
    pallas_call x1, Pallas kernels, block(): pl.pallas_call(block_kernel, out_shape=(shape((128, D), bf16), shape((128...  139 us
    pallas_call x1, Pallas kernels, finish(): pl.pallas_call(final_kernel, out_shape=tuple((jax.ShapeDtypeStruct(*shape...  5.65 us

profile of v5, /device:TPU:0, one launch (start us, length us, event | category | flops | bytes accessed | tf_op | source)
XLA Modules:
  0.0 148.3 jit_solution(6590892433986541534)
XLA Ops:
  1.9 0.1 sine_convert_fusion
  2.0 1.3 broadcast_in_dim.19.refs_4_
  3.3 0.6 broadcast_in_dim.20.refs_5_
  3.9 138.6 %shard_map.323 = (bf16[128,768]{1,0:T(8,128)(2,1)}, bf16[128,768]{1,0:T(8,128)(2,1)}, f32[16,768]{1,0:T(8,128)}, f32[8,768]{1,0:T(8,128)}, bf16[16,768]{1,0:T(8,...) custom-call(s32[1]{0:T(128)S(6)} %copy.38.length_ref, ...), custom_call_target="tpu_custom_call" | custom-call | tf_op jit(solution)/shard_map/pallas_call | solution.py:1060
  142.5 5.7 %shard_map.324 = (bf16[128,768]{1,0:T(8,128)(2,1)}, bf16[128,768]{1,0:T(8,128)(2,1)}, f32[16,768]{1,0:T(8,128)}, f32[96,256]{1,0:T(8,128)}, f32[96,768]{1,0:T(8,...) custom-call(bf16[16,2,2,48,384]{4,3,2,1,0:T(8,128)(2,1)} %get-tuple-, ...), custom_call_target="tpu_custom_call" | custom-call | tf_op jit(solution)/shard_map/pallas_call | solution.py:1169
  (1 shorter events, 0.0 us)
